TPU v7x, 32 devices: a whole 2x2x4 slice. The times are simulated.
32 devices in a mesh: ctx: 2 (over y), fsdp: 16 (over z, x, core).
Axes of the slice: x: 2, y: 2, z: 4, core: 2. Of those that a mesh axis runs over, the one named last changes fastest.
Arguments:
- tokens: bfloat16 [16, 1024, 768], P('fsdp', 'ctx'), may hold values from -6 to 6
- step_embed: bfloat16 [16, 768], P('fsdp'), may hold values from -3 to 3
- block_ids: int32 [16, 4], P('fsdp', 'ctx'), may hold values from 0 to 3, as said below
- cotangent: bfloat16 [16, 1024, 768], P('fsdp', 'ctx'), may hold values from -6 to 6
- project_weight: float32 [768, 2304], P('fsdp'), may hold values from -0.21875 to 0.21875
- project_bias: float32 [2, 768], P(None, 'fsdp'), may hold values from -2 to 2
- output_weight: float32 [768, 768], P('fsdp'), may hold values from -3 to 3
- output_bias: float32 [768], P('fsdp'), may hold values from -2 to 2
- first_gain: float32 [768], P('fsdp'), may hold values from 0.25 to 1.75
- first_shift: float32 [768], P('fsdp'), may hold values from -2 to 2
- up_weight: float32 [768, 3072], P('fsdp'), may hold values from -0.21875 to 0.21875
- up_bias: float32 [3072], P('fsdp'), may hold values from -3 to 3
- down_weight: float32 [3072, 768], P('fsdp'), may hold values from -0.109375 to 0.109375
- down_bias: float32 [768], P('fsdp'), may hold values from -2 to 2
- second_gain: float32 [768], P('fsdp'), may hold values from 0.25 to 1.75
- second_shift: float32 [768], P('fsdp'), may hold values from -2 to 2
Outputs:
- output: float32 [16, 1024, 768], P('fsdp', 'ctx')
- token_grad: float32 [16, 1024, 768], P('fsdp', 'ctx')
- grad_project_weight: float32 [768, 2304], P('fsdp')
- grad_project_bias: float32 [2, 768], P(None, 'fsdp')
- grad_output_weight: float32 [768, 768], P('fsdp')
- grad_output_bias: float32 [768], P('fsdp')
- grad_first_gain: float32 [768], P('fsdp')
- grad_first_shift: float32 [768], P('fsdp')
- grad_up_weight: float32 [768, 3072], P('fsdp')
- grad_up_bias: float32 [3072], P('fsdp')
- grad_down_weight: float32 [3072, 768], P('fsdp')
- grad_down_bias: float32 [768], P('fsdp')
- grad_second_gain: float32 [768], P('fsdp')
- grad_second_shift: float32 [768], P('fsdp')
Inputs may be any that keep to these rules, and one draw needn't show every extreme that they name: `block_ids`: in every sequence each id appears once, and the two blocks stored on one index of ctx have ids adding to 3.
All inputs are finite; a program needn't handle non-finite values.
Results may differ from a plain program's by a relative error of at most 0.019.
The roundings to bfloat16 on the way count: a program that leaves them out, or rounds other values in their place, can miss the bound.
Values may be sent and summed in bfloat16 or wider, within the bound.
No kernel may reach another device: no remote copies, remote signals or barrier semaphores. Data moves between devices by JAX's collectives and lax.ppermute only.
A program may use at most 192 MiB of HBM per device.

v0:
```python
import jax
import jax.numpy as jnp
from jax import lax
from jax.sharding import PartitionSpec as P

HEADS = 12


norm_epsilon = 1e-05
masked_score = -1e30


def layer_norm(values, gain, shift):
    center = values - jnp.mean(values, axis=-1, keepdims=True)
    spread = jnp.mean(center * center, axis=-1, keepdims=True)
    return center * lax.rsqrt(spread + norm_epsilon) * gain + shift


def gelu_exact(values):
    return jax.nn.gelu(values, approximate=False)


def product(left, right):
    return jnp.dot(left, right, preferred_element_type=jnp.float32)


def transpose_left(left, right):
    return lax.dot_general(
        left, right, (((0,), (0,)), ((), ())), preferred_element_type=jnp.float32
    )


def transpose_right(left, right):
    return lax.dot_general(
        left, right, (((1,), (1,)), ((), ())), preferred_element_type=jnp.float32
    )


def column_sum(values):
    return jnp.sum(values.astype(jnp.float32), axis=0)


def shards(
    tokens,
    step_embed,
    block_ids,
    cotangent,
    project_weight,
    project_bias,
    output_weight,
    output_bias,
    first_gain,
    first_shift,
    up_weight,
    up_bias,
    down_weight,
    down_bias,
    second_gain,
    second_shift,
):
    gathered = (
        lax.all_gather(project_weight.astype(jnp.bfloat16), "fsdp", axis=0, tiled=True),
        lax.all_gather(project_bias.astype(jnp.bfloat16), "fsdp", axis=1, tiled=True),
        lax.all_gather(output_weight.astype(jnp.bfloat16), "fsdp", axis=0, tiled=True),
        lax.all_gather(output_bias.astype(jnp.bfloat16), "fsdp", axis=0, tiled=True),
        lax.all_gather(first_gain.astype(jnp.bfloat16), "fsdp", axis=0, tiled=True),
        lax.all_gather(first_shift.astype(jnp.bfloat16), "fsdp", axis=0, tiled=True),
        lax.all_gather(up_weight.astype(jnp.bfloat16), "fsdp", axis=0, tiled=True),
        lax.all_gather(up_bias.astype(jnp.bfloat16), "fsdp", axis=0, tiled=True),
        lax.all_gather(down_weight.astype(jnp.bfloat16), "fsdp", axis=0, tiled=True),
        lax.all_gather(down_bias.astype(jnp.bfloat16), "fsdp", axis=0, tiled=True),
        lax.all_gather(second_gain.astype(jnp.bfloat16), "fsdp", axis=0, tiled=True),
        lax.all_gather(second_shift.astype(jnp.bfloat16), "fsdp", axis=0, tiled=True),
    )
    (
        project_matrix,
        project_offset,
        output_matrix,
        output_offset,
        first_scale,
        first_offset,
        up_matrix,
        up_offset,
        down_matrix,
        down_offset,
        second_scale,
        second_offset,
    ) = gathered
    seq_count, pair_rows, width = tokens.shape
    head_dim = width // HEADS
    pair_width = 2 * head_dim
    pair_count = HEADS // 2
    scale = head_dim ** (-0.5)
    flat_rows = seq_count * pair_rows
    pair_indices = jnp.arange(pair_count, dtype=jnp.int32)

    def head_pair(source, pair_index):
        piece = lax.dynamic_slice_in_dim(source, pair_index * pair_width, pair_width, 2)
        return piece.reshape(seq_count, source.shape[1], 2, head_dim)

    def merge_pairs(stacked):
        return jnp.transpose(stacked, (1, 2, 0, 3)).reshape(flat_rows, width)

    hidden_zero = (tokens.astype(jnp.float32) + step_embed.astype(jnp.float32)[:, None, :]).reshape(
        flat_rows, width
    )
    hidden_zero_low = hidden_zero.astype(jnp.bfloat16)
    offsets = project_offset.astype(jnp.float32)
    bias_row = jnp.concatenate([offsets[0], jnp.zeros_like(offsets[0]), offsets[1]])
    projected = (product(hidden_zero_low, project_matrix) + bias_row).astype(jnp.bfloat16)
    queries = projected[:, :width].reshape(seq_count, pair_rows, width)
    keys_here = projected[:, width : 2 * width].reshape(seq_count, pair_rows, width)
    values_here = projected[:, 2 * width :].reshape(seq_count, pair_rows, width)
    keys_all, values_all, ids_all = (
        lax.all_gather(keys_here, "ctx", axis=1, tiled=True),
        lax.all_gather(values_here, "ctx", axis=1, tiled=True),
        lax.all_gather(block_ids.astype(jnp.bfloat16), "ctx", axis=1, tiled=True),
    )
    block_rows = pair_rows // block_ids.shape[1]
    query_ids = jnp.repeat(block_ids, block_rows, axis=1)
    key_ids = jnp.repeat(ids_all.astype(jnp.int32), block_rows, axis=1)
    allowed = key_ids[:, None, None, :] <= query_ids[:, None, :, None]

    def forward_pair(pair_index):
        query_pair = head_pair(queries, pair_index)
        key_pair = head_pair(keys_all, pair_index)
        value_pair = head_pair(values_all, pair_index)
        scores = (
            jnp.einsum("bqhd,bkhd->bhqk", query_pair, key_pair, preferred_element_type=jnp.float32)
            * scale
        )
        scores = jnp.where(allowed, scores, masked_score)
        peak = jnp.max(scores, axis=-1, keepdims=True)
        expon = jnp.exp(scores - peak)
        totals = jnp.sum(expon, axis=-1, keepdims=True)
        probs = expon / totals
        mixed_pair = jnp.einsum(
            "bhqk,bkhd->bqhd",
            probs.astype(jnp.bfloat16),
            value_pair,
            preferred_element_type=jnp.float32,
        )
        log_total = (peak + jnp.log(totals))[..., 0]
        return (
            mixed_pair.astype(jnp.bfloat16).reshape(seq_count, pair_rows, pair_width),
            log_total,
        )

    mixed_pairs, log_totals = lax.map(forward_pair, pair_indices)
    mixed = merge_pairs(mixed_pairs)
    branch = product(mixed, output_matrix) + output_offset.astype(jnp.float32)
    hidden_one, first_pull = jax.vjp(
        layer_norm,
        hidden_zero + branch,
        first_scale.astype(jnp.float32),
        first_offset.astype(jnp.float32),
    )
    hidden_one_low = hidden_one.astype(jnp.bfloat16)
    inner = product(hidden_one_low, up_matrix) + up_offset.astype(jnp.float32)
    activated, gelu_pull = jax.vjp(gelu_exact, inner)
    activated_low = activated.astype(jnp.bfloat16)
    feed = product(activated_low, down_matrix) + down_offset.astype(jnp.float32)
    result, second_pull = jax.vjp(
        layer_norm,
        hidden_one + feed,
        second_scale.astype(jnp.float32),
        second_offset.astype(jnp.float32),
    )
    project_back, output_back, up_back, down_back = (
        lax.all_gather(project_weight.astype(jnp.bfloat16), "fsdp", axis=0, tiled=True),
        lax.all_gather(output_weight.astype(jnp.bfloat16), "fsdp", axis=0, tiled=True),
        lax.all_gather(up_weight.astype(jnp.bfloat16), "fsdp", axis=0, tiled=True),
        lax.all_gather(down_weight.astype(jnp.bfloat16), "fsdp", axis=0, tiled=True),
    )
    grad_second_in, grad_second_gain, grad_second_shift = second_pull(
        cotangent.reshape(flat_rows, width).astype(jnp.float32)
    )
    feed_grad = grad_second_in.astype(jnp.bfloat16)
    grad_down_bias = column_sum(feed_grad)
    grad_down_weight = transpose_left(activated_low, feed_grad)
    activated_grad = transpose_right(feed_grad, down_back)
    inner_grad = gelu_pull(activated_grad)[0].astype(jnp.bfloat16)
    grad_up_bias = column_sum(inner_grad)
    grad_up_weight = transpose_left(hidden_one_low, inner_grad)
    hidden_one_grad = grad_second_in + transpose_right(inner_grad, up_back)
    grad_first_in, grad_first_gain, grad_first_shift = first_pull(hidden_one_grad)
    branch_grad = grad_first_in.astype(jnp.bfloat16)
    grad_output_bias = column_sum(branch_grad)
    grad_output_weight = transpose_left(mixed, branch_grad)
    mixed_grad = (
        transpose_right(branch_grad, output_back)
        .astype(jnp.bfloat16)
        .reshape(seq_count, pair_rows, width)
    )

    def backward_pair(pair_inputs):
        pair_index, log_total = pair_inputs
        query_pair = head_pair(queries, pair_index)
        key_pair = head_pair(keys_all, pair_index)
        value_pair = head_pair(values_all, pair_index)
        grad_pair = head_pair(mixed_grad, pair_index)
        scores = (
            jnp.einsum("bqhd,bkhd->bhqk", query_pair, key_pair, preferred_element_type=jnp.float32)
            * scale
        )
        probs = jnp.where(allowed, jnp.exp(scores - log_total[..., None]), 0.0)
        prob_grad = jnp.einsum(
            "bqhd,bkhd->bhqk", grad_pair, value_pair, preferred_element_type=jnp.float32
        )
        row_dot = jnp.sum(probs * prob_grad, axis=-1, keepdims=True)
        score_grad = (probs * (prob_grad - row_dot)).astype(jnp.bfloat16)
        query_grad = (
            jnp.einsum("bhqk,bkhd->bqhd", score_grad, key_pair, preferred_element_type=jnp.float32)
            * scale
        )
        key_grad = (
            jnp.einsum(
                "bhqk,bqhd->bkhd", score_grad, query_pair, preferred_element_type=jnp.float32
            )
            * scale
        )
        value_grad = jnp.einsum(
            "bhqk,bqhd->bkhd",
            probs.astype(jnp.bfloat16),
            grad_pair,
            preferred_element_type=jnp.float32,
        )
        return (
            query_grad.astype(jnp.bfloat16).reshape(seq_count, pair_rows, pair_width),
            key_grad.reshape(seq_count, key_pair.shape[1], pair_width),
            value_grad.reshape(seq_count, key_pair.shape[1], pair_width),
        )

    query_grads, key_partial, value_partial = lax.map(backward_pair, (pair_indices, log_totals))
    key_sums, value_sums = (
        lax.psum_scatter(
            key_partial.astype(jnp.bfloat16), "ctx", scatter_dimension=2, tiled=True
        ).astype(jnp.float32),
        lax.psum_scatter(
            value_partial.astype(jnp.bfloat16), "ctx", scatter_dimension=2, tiled=True
        ).astype(jnp.float32),
    )
    key_grads = key_sums.astype(jnp.bfloat16)
    value_grads = value_sums.astype(jnp.bfloat16)
    project_grad = jnp.concatenate(
        [merge_pairs(query_grads), merge_pairs(key_grads), merge_pairs(value_grads)], axis=1
    )
    grad_project_bias = jnp.stack(
        [column_sum(project_grad[:, :width]), column_sum(project_grad[:, 2 * width :])]
    )
    grad_project_weight = transpose_left(hidden_zero_low, project_grad)
    input_grad = grad_first_in + transpose_right(project_grad, project_back)
    shares = (
        lax.psum_scatter(
            grad_project_weight.astype(jnp.bfloat16), "fsdp", scatter_dimension=0, tiled=True
        ).astype(jnp.float32),
        lax.psum_scatter(
            grad_project_bias.astype(jnp.bfloat16), "fsdp", scatter_dimension=1, tiled=True
        ).astype(jnp.float32),
        lax.psum_scatter(
            grad_output_weight.astype(jnp.bfloat16), "fsdp", scatter_dimension=0, tiled=True
        ).astype(jnp.float32),
        lax.psum_scatter(
            grad_output_bias.astype(jnp.bfloat16), "fsdp", scatter_dimension=0, tiled=True
        ).astype(jnp.float32),
        lax.psum_scatter(
            grad_first_gain.astype(jnp.bfloat16), "fsdp", scatter_dimension=0, tiled=True
        ).astype(jnp.float32),
        lax.psum_scatter(
            grad_first_shift.astype(jnp.bfloat16), "fsdp", scatter_dimension=0, tiled=True
        ).astype(jnp.float32),
        lax.psum_scatter(
            grad_up_weight.astype(jnp.bfloat16), "fsdp", scatter_dimension=0, tiled=True
        ).astype(jnp.float32),
        lax.psum_scatter(
            grad_up_bias.astype(jnp.bfloat16), "fsdp", scatter_dimension=0, tiled=True
        ).astype(jnp.float32),
        lax.psum_scatter(
            grad_down_weight.astype(jnp.bfloat16), "fsdp", scatter_dimension=0, tiled=True
        ).astype(jnp.float32),
        lax.psum_scatter(
            grad_down_bias.astype(jnp.bfloat16), "fsdp", scatter_dimension=0, tiled=True
        ).astype(jnp.float32),
        lax.psum_scatter(
            grad_second_gain.astype(jnp.bfloat16), "fsdp", scatter_dimension=0, tiled=True
        ).astype(jnp.float32),
        lax.psum_scatter(
            grad_second_shift.astype(jnp.bfloat16), "fsdp", scatter_dimension=0, tiled=True
        ).astype(jnp.float32),
    )
    summed = (
        lax.psum(shares[0].astype(jnp.bfloat16), "ctx").astype(jnp.float32),
        lax.psum(shares[1].astype(jnp.bfloat16), "ctx").astype(jnp.float32),
        lax.psum(shares[2].astype(jnp.bfloat16), "ctx").astype(jnp.float32),
        lax.psum(shares[3].astype(jnp.bfloat16), "ctx").astype(jnp.float32),
        lax.psum(shares[4].astype(jnp.bfloat16), "ctx").astype(jnp.float32),
        lax.psum(shares[5].astype(jnp.bfloat16), "ctx").astype(jnp.float32),
        lax.psum(shares[6].astype(jnp.bfloat16), "ctx").astype(jnp.float32),
        lax.psum(shares[7].astype(jnp.bfloat16), "ctx").astype(jnp.float32),
        lax.psum(shares[8].astype(jnp.bfloat16), "ctx").astype(jnp.float32),
        lax.psum(shares[9].astype(jnp.bfloat16), "ctx").astype(jnp.float32),
        lax.psum(shares[10].astype(jnp.bfloat16), "ctx").astype(jnp.float32),
        lax.psum(shares[11].astype(jnp.bfloat16), "ctx").astype(jnp.float32),
    )
    return (
        result.reshape(seq_count, pair_rows, width),
        input_grad.reshape(seq_count, pair_rows, width),
        summed[0],
        summed[1],
        summed[2],
        summed[3],
        summed[4],
        summed[5],
        summed[6],
        summed[7],
        summed[8],
        summed[9],
        summed[10],
        summed[11],
    )


def solution(mesh):
    return jax.shard_map(
        shards,
        mesh=mesh,
        in_specs=(
            P("fsdp", "ctx", None),
            P("fsdp", None),
            P("fsdp", "ctx"),
            P("fsdp", "ctx", None),
            P("fsdp", None),
            P(None, "fsdp"),
            P("fsdp", None),
            P("fsdp"),
            P("fsdp"),
            P("fsdp"),
            P("fsdp", None),
            P("fsdp"),
            P("fsdp", None),
            P("fsdp"),
            P("fsdp"),
            P("fsdp"),
        ),
        out_specs=(
            P("fsdp", "ctx", None),
            P("fsdp", "ctx", None),
            P("fsdp", None),
            P(None, "fsdp"),
            P("fsdp", None),
            P("fsdp"),
            P("fsdp"),
            P("fsdp"),
            P("fsdp", None),
            P("fsdp"),
            P("fsdp", None),
            P("fsdp"),
            P("fsdp"),
            P("fsdp"),
        ),
        check_vma=False,
    )
```

profile of v0, /device:TPU:0, one launch (start us, length us, event | category | flops | bytes accessed | tf_op | source)
XLA Modules:
  0.0 857.7 jit_solution(12785414366772415956)
XLA Ops:
  7.2 1.7 convert_element_type.245
  9.7 23.0 %all-gather.2 = bf16[16,48,2]{1,2,0:T(2,128)(2,1)S(1)} all-gather(bf16[1,48,2]{1,2,0:T(2,128)(2,1)S(1)} %convert_bitcast_fusion.1), channel_id=1, replica_groups=mesh['ctx'=2,'fsdp'=16] {'fsdp'}, dimensions={0}, use_global_device_ids=true | all-gather | bytes 3264 | tf_op jit(solution)/shard_map/all_gather | solution.py:63
  33.5 27.3 %all-gather.10.cloned.1.call-done = bf16[768,2304]{1,0:T(8,128)(2,1)} async-done(((bf16[48,2304]{1,0:T(8,128)(2,1)}), bf16[768,2304]{1,0:T(8,128)(2,1)}) %all-gather.10.cloned.1.call-update) | async-done | bytes 3538960 | tf_op jit(solution)/shard_map/all_gather | solution.py:62
  60.8 4.2 fusion.23
  74.6 59.7 %all-reduce.16 = (bf16[768]{0:T(1024)(128)(2,1)S(1)}, bf16[768]{0:T(1024)(128)(2,1)S(1)}, bf16[768]{0:T(1024)(128)(2,1)S(1)}, bf16[3072]{0:T(1024)(128)(2,1)S(1)...) all-reduce(bf16[768]{0:T(1024)(128)(2,1)S(1)} %dynamic-update-slice, ...), channel_id=1, replica_groups=mesh['ctx'=2,'fsdp'=16] {'fsdp'}, use_global_device_ids=true, to_apply=%add.1 | all-reduce | flops 6912 | bytes 27648
  134.3 5.4 all-reduce
  141.1 1.7 copy.54
  142.9 1.7 copy.56
  145.6 41.9 %while.28 = (s32[]{:T(128)}, bf16[6,1,512,128]{2,3,1,0:T(8,128)(2,1)}, f32[6,1,2,512]{3,2,1,0:T(2,128)S(1)}, s32[6]{0:T(128)S(1)}, bf16[1,1024,768]{1,2,0:T(8,12...) while((s32[]{:T(128)}, ...), condition=%wide.region_3.4_spmd.clone, body=%wide.region_0.3_spmd.clone.sunk | while | flops 281607168 | bytes 17078980 | solution.py:149
  150.4 1.5 fusion.102
  157.4 1.5 fusion.102
  164.4 1.5 fusion.102
  171.4 1.5 fusion.102
  178.4 1.5 fusion.102
  185.4 1.5 fusion.102
  187.5 3.2 fusion.45
  192.2 26.3 %all-gather.14.cloned.1.call-done = bf16[768,3072]{1,0:T(8,128)(2,1)} async-done(((bf16[48,3072]{1,0:T(8,128)(2,1)}), bf16[768,3072]{1,0:T(8,128)(2,1)}) %all-gather.14.cloned.1.call-update) | async-done | bytes 4718608 | tf_op jit(solution)/shard_map/all_gather | solution.py:68
  218.5 21.0 %multiply_convert_fusion.1 = (bf16[512,3072]{1,0:T(8,128)(2,1)}, f32[512,3072]{1,0:T(8,128)}, f32[512,3072]{1,0:T(8,128)}) fusion(f32[3072]{0:T(1024)S(1)} %convert_element_type.262, bf16[768,3072]{1,0:T(8,128)(2,1)} %all-gather.14.cloned.1.call-done, f32[512,768]{1,0:T(8,128)} %copy-done.8, f32[768]{0:T(1024)S(1)} %convert_element_type.258, ...), kind=kOutput, calls=%fused_computation.40 | convolution fusion | flops 2521694208 | bytes 22042624 | tf_op jit(solution)/shard_map/dot_general | solution.py:24
  239.5 33.6 %all-gather.16.cloned.1.call-done = bf16[3072,768]{1,0:T(8,128)(2,1)} async-done(((bf16[192,768]{1,0:T(8,128)(2,1)}), bf16[3072,768]{1,0:T(8,128)(2,1)}) %all-gather.16.cloned.1.call-update) | async-done | bytes 4718608 | tf_op jit(solution)/shard_map/all_gather | solution.py:70
  273.1 6.5 fusion.46
  281.6 1.7 copy-done.20
  283.3 9.2 %fusion.38 = (bf16[3072]{0:T(1024)(128)(2,1)S(1)}, bf16[512,3072]{1,0:T(8,128)(2,1)}) fusion(f32[512,3072]{1,0:T(8,128)} %get-tuple-element.341, f32[512,3072]{1,0:T(8,128)} %get-tuple-element.357, f32[3072]{0:T(1024)S(1)} %convert_element_type.262, bf16[512,768]{1,0:T(8,128)(2,1)S(1)} %get-tuple-element.331, bf16[3072,768]{1,0:T(8,128)(2,1)S(1)} %copy-done.20), kind=kOutput, calls=%fused_computation.115 | convolution fusion | flops 2441081856 | bytes 21252096 | tf_op jit(solution)/shard_map/dot_general | solution.py:34
  292.5 5.1 multiply_reduce_fusion.1
  300.6 1.7 fusion.28
  303.3 101.9 %while.29 = (s32[]{:T(128)}, bf16[6,1,512,128]{2,3,1,0:T(8,128)(2,1)}, bf16[6,1,1024,128]{2,3,1,0:T(8,128)(2,1)}, bf16[6,1,1024,128]{2,3,1,0:T(8,128)(2,1)}, s32...) while((s32[]{:T(128)}, ...), condition=%wide.region_14.15_spmd.clone, body=%wide.region_12.14_spmd.clone.sunk | while | flops 687733760 | bytes 68062520 | solution.py:234
  305.8 2.7 fusion.113
  310.9 4.1 multiply_reduce_fusion.6
  315.0 1.4 multiply_convert_fusion.3
  322.7 2.7 fusion.113
  327.8 4.1 multiply_reduce_fusion.6
  331.9 1.4 multiply_convert_fusion.3
  339.7 2.7 fusion.113
  344.8 4.1 multiply_reduce_fusion.6
  348.9 1.4 multiply_convert_fusion.3
  356.6 2.7 fusion.113
  361.7 4.1 multiply_reduce_fusion.6
  365.8 1.4 multiply_convert_fusion.3
  373.6 2.7 fusion.113
  378.6 4.1 multiply_reduce_fusion.6
  382.8 1.4 multiply_convert_fusion.3
  390.5 2.7 fusion.113
  395.6 4.1 multiply_reduce_fusion.6
  399.7 1.4 multiply_convert_fusion.3
  406.0 3.2 convolution_convert_fusion.3
  409.3 7.0 convolution_convert_fusion
  416.4 1.3 copy-done.10
  417.7 6.5 convolution_convert_fusion.1
  424.5 5.4 reduce-scatter.12.cloned.1.call-done
  430.0 29.0 %reduce-scatter.10.cloned.1.call-done = bf16[6,1,512,128]{2,3,1,0:T(8,128)(2,1)} async-done(((bf16[6,1,1024,128]{2,3,1,0:T(8,128)(2,1)}), bf16[6,1,512,128]{2,3,1,0:T(8,128)(2,1)}) %reduce-scatter.10.cloned.1.call-update) | async-done | bytes 786448 | tf_op jit(solution)/shard_map/reduce_scatter | solution.py:236
  459.0 5.4 convolution_convert_fusion.2
  464.5 1.4 bitcast_reduce_fusion.1
  468.9 61.3 %all-reduce.15 = (bf16[768]{0:T(1024)(128)(2,1)S(1)}, bf16[768]{0:T(1024)(128)(2,1)S(1)}, bf16[768]{0:T(1024)(128)(2,1)S(1)}, bf16[768]{0:T(1024)(128)(2,1)S(1)}...) all-reduce(bf16[768]{0:T(1024)(128)(2,1)S(1)} %dynamic-update-slice, ...), channel_id=1, replica_groups=mesh['ctx'=2,'fsdp'=16] {'fsdp'}, use_global_device_ids=true, to_apply=%add.7 | all-reduce | flops 8448 | bytes 33792
  530.8 68.3 %reduce-scatter.20.cloned.1.call-done = bf16[192,768]{1,0:T(8,128)(2,1)} async-done(((bf16[3072,768]{1,0:T(8,128)(2,1)}), bf16[192,768]{1,0:T(8,128)(2,1)}) %reduce-scatter.20.cloned.1.call-update) | async-done | bytes 294928 | tf_op jit(solution)/shard_map/reduce_scatter | solution.py:278
  599.1 79.0 %reduce-scatter.18.cloned.1.call-done = bf16[48,3072]{1,0:T(8,128)(2,1)} async-done(((bf16[768,3072]{1,0:T(8,128)(2,1)}), bf16[48,3072]{1,0:T(8,128)(2,1)}) %reduce-scatter.18.cloned.1.call-update) | async-done | bytes 294928 | tf_op jit(solution)/shard_map/reduce_scatter | solution.py:272
  678.1 70.9 %reduce-scatter.14.cloned.1.call-done = bf16[48,2304]{1,0:T(8,128)(2,1)} async-done(((bf16[768,2304]{1,0:T(8,128)(2,1)}), bf16[48,2304]{1,0:T(8,128)(2,1)}) %reduce-scatter.14.cloned.1.call-update) | async-done | bytes 221200 | tf_op jit(solution)/shard_map/reduce_scatter | solution.py:254
  749.0 1.4 add_bitcast_fusion.1
  750.5 5.9 add_bitcast_fusion
  756.4 49.2 %reduce-scatter.22.cloned.1.call-done = bf16[48,2]{1,0:T(8,128)(2,1)} async-done(((bf16[768,2]{1,0:T(8,128)(2,1)}), bf16[48,2]{1,0:T(8,128)(2,1)}) %reduce-scatter.22.cloned.1.call-update) | async-done | bytes 208
  806.4 4.9 all-reduce.17
  815.5 28.5 %all-reduce.21.cloned.1.call-done = (bf16[48,2304]{1,0:T(8,128)(2,1)}, bf16[48,768]{1,0:T(8,128)(2,1)}, bf16[48,3072]{1,0:T(8,128)(2,1)}, bf16[192,768]{1,0:T(8,128)(2,1)}) async-done(((bf16[48,2304]{1,0:T(8,128)(2,1)}, bf16[48,768]{1,0:T(8,128)(2,1)}, bf16[48,3072]{1,0:T(8,128)(2,1)}, bf16[192,768]{1,0:T(8,128)(2,1)}), (bf16[48,2304]{1,0:T(8,128)(2,1)}, bf16[48,768]{1,0:T(8,128)(2,1)}, ...) | async-done | bytes 884752 | tf_op jit(solution)/shard_map/psum | solution.py:292
  844.0 1.8 convert_element_type.292
  845.8 1.8 convert_element_type.295
  847.6 1.7 convert_element_type.280
  849.4 1.6 convert_element_type.285
  (346 shorter events, 104.1 us)
Async XLA Ops:
  7.2 53.6 %all-gather.10.cloned.1.call-start = ((), (), s32[]{:S(2)}) async-start(), calls=%async_computation.7 | async-start | bytes 3760128 | tf_op jit(solution)/shard_map/all_gather | solution.py:62
  9.0 132.1 %all-gather.18.cloned.1.call-start = ((), (), s32[]{:S(2)}) async-start(), calls=%async_computation.17 | async-start | bytes 2359296 | tf_op jit(solution)/shard_map/all_gather | solution.py:116
  65.0 2.3 copy-start.17
  65.1 3.0 copy-start.15
  65.1 3.8 copy-start.16
  65.1 4.7 copy-start.24
  65.1 4.7 copy-start.25
  65.1 4.7 copy-start.26
  65.1 4.7 copy-start.27
  65.1 4.7 copy-start.28
  65.1 4.7 copy-start.18
  65.2 6.6 copy-start.23
  65.2 6.6 copy-start.30
  65.2 7.2 copy-start.19
  66.5 76.3 %all-gather.20.cloned.1.call-start = ((), (), s32[]{:S(2)}) async-start(), calls=%async_computation.18 | async-start | bytes 2359296 | tf_op jit(solution)/shard_map/all_gather | solution.py:115
  67.3 120.2 %all-gather.12.cloned.1.call-start = ((), (), s32[]{:S(2)}) async-start(), calls=%async_computation.8 | async-start | bytes 1253376 | tf_op jit(solution)/shard_map/all_gather | solution.py:64
  68.0 150.5 %all-gather.14.cloned.1.call-start = ((), (), s32[]{:S(2)}) async-start(), calls=%async_computation.9 | async-start | bytes 5013504 | tf_op jit(solution)/shard_map/all_gather | solution.py:68
  68.8 204.2 %all-gather.16.cloned.1.call-start = ((), (), s32[]{:S(2)}) async-start(), calls=%async_computation.10 | async-start | bytes 5013504 | tf_op jit(solution)/shard_map/all_gather | solution.py:70
  69.6 360.3 %reduce-scatter.12.cloned.1.call-start = ((), (), s32[]{:S(2)}) async-start(), calls=%async_computation.12 | async-start | bytes 2359296 | tf_op jit(solution)/shard_map/reduce_scatter | solution.py:239
  187.5 4.7 copy-start.1
  190.7 1.1 copy-start.8
  273.1 6.9 copy-start.4
  280.7 2.6 copy-start.20
  281.4 11.1 %slice-start = ((s8[4718592]{0:T(1024)(128)(4,1)}), s8[4194304]{0:T(1024)(128)(4,1)S(1)}, s32[]{:S(2)}) async-start(s8[4718592]{0:T(1024)(128)(4,1)} %bitcast.216), calls=%async_computation.21 | async-start | bytes 8388608
  281.6 10.9 %copy-start.12 = (bf16[512,768]{1,0:T(8,128)(2,1)}, bf16[512,768]{1,0:T(8,128)(2,1)S(1)}, u32[]{:S(2)}) copy-start(bf16[512,768]{1,0:T(8,128)(2,1)S(1)} %get-tuple-element.331) | copy-start | bytes 2359300
  283.3 9.2 %copy-start.9 = (f32[512,768]{1,0:T(8,128)S(1)}, f32[512,768]{1,0:T(8,128)}, u32[]{:S(2)}) copy-start(f32[512,768]{1,0:T(8,128)} %copy-done.8) | copy-start | bytes 4718596
  283.3 9.2 %slice-start.1 = ((s8[4718592]{0:T(1024)(128)(4,1)}), s8[524288]{0:T(1024)(128)(4,1)S(1)}, s32[]{:S(2)}) async-start(s8[4718592]{0:T(1024)(128)(4,1)} %bitcast.216), calls=%async_computation.22 | async-start | bytes 1048576
  297.6 2.9 copy-start.21
  298.3 1.2 copy-start.6
  299.7 0.9 copy-start.14
  303.5 1.4 copy-start.2
  310.9 4.1 copy-start
  318.2 2.3 copy-start.3
  320.4 1.4 copy-start.2
  327.8 4.1 copy-start
  335.1 2.3 copy-start.3
  337.4 1.4 copy-start.2
  344.8 4.1 copy-start
  352.1 2.3 copy-start.3
  354.3 1.4 copy-start.2
  361.7 4.1 copy-start
  369.0 2.3 copy-start.3
  371.3 1.4 copy-start.2
  378.6 4.1 copy-start
  385.9 2.3 copy-start.3
  388.2 1.4 copy-start.2
  395.6 4.1 copy-start
  402.9 2.3 copy-start.3
  405.2 4.1 copy-start.13
  405.2 53.8 %reduce-scatter.10.cloned.1.call-start = ((), (), s32[]{:S(2)}) async-start(), calls=%async_computation.11 | async-start | bytes 2359296 | tf_op jit(solution)/shard_map/reduce_scatter | solution.py:236
  405.9 124.8 %reduce-scatter.16.cloned.1.call-start = ((), (), s32[]{:S(2)}) async-start(), calls=%async_computation.14 | async-start | bytes 1253376 | tf_op jit(solution)/shard_map/reduce_scatter | solution.py:260
  409.2 189.9 %reduce-scatter.20.cloned.1.call-start = ((), (), s32[]{:S(2)}) async-start(), calls=%async_computation.16 | async-start | bytes 5013504 | tf_op jit(solution)/shard_map/reduce_scatter | solution.py:278
  416.3 1.4 copy-start.10
  416.3 261.8 %reduce-scatter.18.cloned.1.call-start = ((), (), s32[]{:S(2)}) async-start(), calls=%async_computation.15 | async-start | bytes 5013504 | tf_op jit(solution)/shard_map/reduce_scatter | solution.py:272
  424.2 34.8 %copy-start.22 = (bf16[1,512,768]{2,1,0:T(8,128)(2,1)S(1)}, bf16[1,512,768]{2,1,0:T(8,128)(2,1)}, u32[]{:S(2)}) copy-start(bf16[1,512,768]{2,1,0:T(8,128)(2,1)} %param.20) | copy-start | bytes 2359300
  424.2 324.8 %reduce-scatter.14.cloned.1.call-start = ((), (), s32[]{:S(2)}) async-start(), calls=%async_computation.13 | async-start | bytes 3760128 | tf_op jit(solution)/shard_map/reduce_scatter | solution.py:254
  464.4 1.5 copy-start.11
  464.4 2.7 copy-start.29
  464.4 2.7 copy-start.5
  464.5 341.1 %reduce-scatter.22.cloned.1.call-start = ((), (), s32[]{:S(2)}) async-start(), calls=%async_computation.19 | async-start | bytes 208896
  467.0 377.0 %all-reduce.21.cloned.1.call-start = ((), (), s32[]{:S(2)}) async-start(), calls=%async_computation.20 | async-start | bytes 1769472 | tf_op jit(solution)/shard_map/psum | solution.py:292
  467.3 283.2 %copy-start.7 = (f32[512,768]{1,0:T(8,128)S(1)}, f32[512,768]{1,0:T(8,128)}, u32[]{:S(2)}) copy-start(f32[512,768]{1,0:T(8,128)} %copy-done.6) | copy-start | bytes 4718596
Sparse Core Ops, SparseCore 0:
  10.9 49.8 all-gather.9
  66.6 26.2 all-gather.17
  95.0 27.2 all-gather.19
  125.0 38.3 all-gather.11
  166.1 52.3 all-gather.13
  221.2 51.7 all-gather.15
  405.3 24.6 reduce-scatter.11
  432.9 26.0 reduce-scatter.9
  462.6 58.1 reduce-scatter.15
  524.5 74.5 reduce-scatter.19
  603.4 74.6 reduce-scatter.17
  681.8 67.1 reduce-scatter.13
  753.1 52.4 reduce-scatter.21
  807.9 36.0 all-reduce.20
where the time goes:
time: 863 us; the launch traced here: 858 us
  waiting for transfers between devices  419 us (49%)
  blocking collectives  154 us (18%)
  matrix products  150 us (17%)
  local copies, waits for them, and re-layouts  63.7 us (7%)
  other arithmetic  42.3 us (5%)
  between operations  18.2 us (2%)
  loops' own time  8.8 us (1%)
    unnamed x3, blocking collectives  126 us
    reduce_scatter x1, waiting for transfers between devices, shards(): lax.psum_scatter(grad_up_weight.astype(jnp.bfloat16), 'fsdp', scatter_dim...  79 us
    reduce_scatter x1, waiting for transfers between devices, shards(): lax.psum_scatter(grad_project_weight.astype(jnp.bfloat16), 'fsdp', scatte...  70.9 us
    reduce_scatter x1, waiting for transfers between devices, shards(): lax.psum_scatter(grad_down_weight.astype(jnp.bfloat16), 'fsdp', scatter_d...  68.3 us
    unnamed x15, waiting for transfers between devices  50.7 us
    dot_general x4, matrix products, product(): return jnp.dot(left, right, preferred_element_type=jnp.float32)  35 us
    all_gather x1, waiting for transfers between devices, shards(): lax.all_gather(down_weight.astype(jnp.bfloat16), 'fsdp', axis=0, tiled=True)  33.6 us
    reduce_scatter x1, waiting for transfers between devices, shards(): lax.psum_scatter(key_partial.astype(jnp.bfloat16), 'ctx', scatter_dimensi...  29 us
  transfers between devices with their start and end apart: 14, of which 10 were waited for; matrix products, arithmetic and copies ran while one was open for 13% of the time, Pallas kernels for 0%

commit v1 on v0

--- a/solution.py
+++ b/solution.py
@@ -1,6 +1,10 @@
+import functools
+
 import jax
 import jax.numpy as jnp
 from jax import lax
+from jax.experimental import pallas as pl
+from jax.experimental.pallas import tpu as pltpu
 from jax.sharding import PartitionSpec as P
 
 HEADS = 12
@@ -320,9 +324,971 @@
     )
 
 
+BF = jnp.bfloat16
+F32 = jnp.float32
+LOG2E = 1.4426950408889634
+VMEM_LIMIT = 60 * 1024 * 1024
+UNIT = 1.15e9
+LIGHT = 0.3
+NT = (((1,), (1,)), ((), ()))
+TN = (((0,), (0,)), ((), ()))
+BLOCK = 256
+SOFT = 32
+SOFT_BACK = 16
+NORM = 128
+
+
+def nn_dot(left, right):
+    return jnp.dot(left, right, preferred_element_type=F32)
+
+
+def nt_dot(left, right):
+    return lax.dot_general(left, right, NT, preferred_element_type=F32)
+
+
+def tn_dot(left, right):
+    return lax.dot_general(left, right, TN, preferred_element_type=F32)
+
+
+def call(weight, kernel, grid, in_specs, outs, scratch, args, aliases={}):
+    return pl.pallas_call(
+        kernel,
+        grid_spec=pltpu.PrefetchScalarGridSpec(
+            num_scalar_prefetch=1,
+            grid=grid,
+            in_specs=in_specs,
+            out_specs=[spec for spec, _, _ in outs],
+            scratch_shapes=scratch,
+        ),
+        out_shape=[jax.ShapeDtypeStruct(shape, dtype) for _, shape, dtype in outs],
+        input_output_aliases=aliases,
+        compiler_params=pltpu.CompilerParams(vmem_limit_bytes=VMEM_LIMIT),
+        cost_estimate=pl.CostEstimate(flops=int(weight * UNIT), bytes_accessed=1, transcendentals=0),
+    )(*args)
+
+
+def tile(shape, index):
+    return pl.BlockSpec(shape, lambda i, info: index(i, info))
+
+
+def fixed(shape):
+    return pl.BlockSpec(shape, lambda i, info: (0,) * len(shape), pipeline_mode=pl.Buffered(1))
+
+
+PIECES, BLOCKS, IDS, SLOTS, CTX, CORE, DOWN, PLACES, ZS = 0, 16, 32, 36, 40, 41, 42, 58, 66
+BIAS_Q, BIAS_V, BIAS_O, GAIN_1, SHIFT_1, BIAS_D, GAIN_2, SHIFT_2, BIAS_U = range(9)
+
+
+def row(ref, at):
+    return ref[at : at + 1, :]
+
+
+def put_rows(info, pieces, target, rows, base=0):
+    at = 0
+    for piece in pieces:
+        for start in range(0, piece.shape[0], rows):
+            place = pl.multiple_of(info[base + at] * rows, 16)
+            target[pl.ds(place, rows), :] = piece[start : start + rows, :]
+            at += 1
+
+
+def permute_rows(info, base, source, keep, send, lanes, rows):
+    for at in range(16):
+        target = keep if at < 8 else send
+        place = pl.multiple_of(info[base + at] * rows, 16)
+        start = at % 8 * rows
+        target[start : start + rows, lanes] = source[pl.ds(place, rows), :]
+
+
+def by_rows(rows, body, chunk):
+    def step(at, carry):
+        return body(pl.ds(pl.multiple_of(at * chunk, chunk), chunk), carry)
+
+    return functools.partial(lax.fori_loop, 0, rows // chunk, step)
+
+
+def fold(values):
+    total = values[:8]
+    for start in range(8, values.shape[0], 8):
+        total = total + values[start : start + 8]
+    return total
+
+
+def mean_last(values):
+    return jnp.mean(values, axis=-1, keepdims=True)
+
+
+def two_heads(values, lane):
+    zero = jnp.zeros_like(values)
+    return jnp.concatenate([jnp.where(lane < 64, values, zero), jnp.where(lane < 64, zero, values)], axis=0)
+
+
+def attend_call(info, pair, pairs, tokens, pieces, vectors):
+    first = vectors is None
+    half_rows, width = tokens[0].shape
+    half_rows = half_rows if first else half_rows // 2
+    length = 2 * half_rows
+    piece_rows = pieces[0].shape[0] // 4
+    count = len(pieces)
+    part = BLOCK
+    specs = [fixed(array.shape) for array in tokens]
+    specs += [tile((4 * piece_rows, 384), lambda i, info: (0, pair + i)) for _ in pieces]
+    args = [*tokens, *pieces]
+    if first:
+        specs += [
+            pl.BlockSpec((4 * piece_rows, 128), lambda i, info: (0, 3 * width // 256), pipeline_mode=pl.Buffered(1))
+            for _ in pieces
+        ]
+        args += pieces
+    else:
+        specs += [fixed(vectors.shape)]
+        args += [vectors]
+
+    def kernel(info, *rest):
+        token_refs, rest = rest[: len(tokens)], rest[len(tokens) :]
+        piece_refs, rest = rest[:count], rest[count:]
+        at_pair = pl.program_id(0)
+        if first:
+            small_refs, rest = rest[:count], rest[count:]
+            qkv_ref, out_own, out_peer, lse_ref, low_ref, vec_ref, weight, stats, mixed, small = rest
+            own_ref, peer_ref, step_ref = token_refs
+
+            @pl.when(at_pair == 0)
+            def _():
+                put_rows(info, small_refs, small, piece_rows)
+                vec_ref[...] = small[...].astype(F32).T[:16, :]
+                for slot in range(4):
+                    source = own_ref if slot < 2 else peer_ref
+                    entries = source[slot % 2 * BLOCK : (slot % 2 + 1) * BLOCK, :].astype(F32)
+                    rows = pl.ds(pl.multiple_of(info[IDS + slot] * BLOCK, BLOCK), BLOCK)
+                    low_ref[rows, :] = (entries + step_ref[...].astype(F32)).astype(BF)
+        else:
+            vec_ref, qkv_ref, out_own, out_peer, lse_ref, weight, stats, mixed = rest
+            low_ref = token_refs[0]
+        put_rows(info, piece_refs, weight, piece_rows)
+        lanes = pl.ds(pl.multiple_of(info[CTX] * (width // 2) + 128 * (pair + at_pair), 128), 128)
+        query_bias = vec_ref[BIAS_Q : BIAS_Q + 1, lanes]
+        value_bias = vec_ref[BIAS_V : BIAS_V + 1, lanes]
+        for at in range(2):
+            rows = slice(half_rows * at, half_rows * (at + 1))
+            result = nn_dot(low_ref[rows, :], weight[...])
+            qkv_ref[rows, :128] = (result[:, :128] + query_bias).astype(BF) * jnp.asarray(0.125, BF)
+            qkv_ref[rows, 128:256] = result[:, 128:256].astype(BF)
+            qkv_ref[rows, 256:] = (result[:, 256:] + value_bias).astype(BF)
+        lane = lax.broadcasted_iota(jnp.int32, (part, 128), 1)
+        for at in range(4):
+            extent = BLOCK * (at + 1)
+            rows = slice(at * BLOCK, extent)
+            query = two_heads(qkv_ref[rows, :128], lane)
+            scores = nt_dot(query, qkv_ref[:extent, 128:256])
+            peak = jnp.max(scores, axis=-1, keepdims=True)
+            expon = jnp.exp2((scores - peak) * LOG2E)
+            total = jnp.sum(expon, axis=-1, keepdims=True)
+            result = nn_dot(expon.astype(BF), qkv_ref[:extent, 256:]) * (1.0 / total)
+            logs = (peak + jnp.log(total)) * LOG2E
+            places = pl.ds(pl.multiple_of(info[SLOTS + at] * BLOCK, BLOCK), BLOCK)
+            mixed[places, :] = jnp.where(lane < 64, result[:part], result[part:]).astype(BF)
+            stats[rows, :] = jnp.where(lane == 0, logs[:part], logs[part:])
+        out_own[...] = mixed[:half_rows, :]
+        out_peer[...] = mixed[half_rows:, :]
+        lse_ref[...] = stats[...].T[:8, :]
+
+    outs = [
+        (tile((length, 384), lambda i, info: (0, i)), (length, 384 * pairs), BF),
+        (tile((half_rows, 128), lambda i, info: (0, i)), (half_rows, 128 * pairs), BF),
+        (tile((half_rows, 128), lambda i, info: (0, i)), (half_rows, 128 * pairs), BF),
+        (tile((8, length), lambda i, info: (i, 0)), (8 * pairs, length), F32),
+    ]
+    scratch = [pltpu.VMEM((width, 384), BF), pltpu.VMEM((length, 128), F32), pltpu.VMEM((length, 128), BF)]
+    if first:
+        outs += [(fixed((length, width)), (length, width), BF), (fixed((16, width)), (16, width), F32)]
+        scratch += [pltpu.VMEM((width, 128), BF)]
+    return call(LIGHT, kernel, (pairs,), specs, outs, scratch, (info, *args))
+
+
+def attend_back_call(info, pair, qkv, own_grad, peer_grad, lse):
+    length = qkv.shape[0]
+    pairs = qkv.shape[1] // 384
+    half_rows = length // 2
+    part = BLOCK
+
+    def kernel(info, qkv_ref, own_ref, peer_ref, lse_ref, out_ref, sums_ref, grads, dk, dv):
+        lane = lax.broadcasted_iota(jnp.int32, (part, 128), 1)
+        for slot in range(4):
+            source = own_ref if slot < 2 else peer_ref
+            place = pl.multiple_of(info[IDS + slot] * BLOCK, BLOCK)
+            grads[pl.ds(place, BLOCK), :] = source[slot % 2 * BLOCK : (slot % 2 + 1) * BLOCK, :]
+        for at in range(3, -1, -1):
+            extent = BLOCK * (at + 1)
+            rows = slice(at * BLOCK, extent)
+            query = two_heads(qkv_ref[rows, :128], lane)
+            grad = two_heads(grads[rows, :], lane)
+            logs = jnp.concatenate([lse_ref[0:1, rows], lse_ref[1:2, rows]], axis=1)
+            probs = jnp.exp2(nt_dot(qkv_ref[:extent, 128:256], query) * LOG2E - logs)
+            prob_grad = nt_dot(qkv_ref[:extent, 256:], grad)
+            delta = jnp.sum(probs * prob_grad, axis=0, keepdims=True)
+            score_grad = (probs * (prob_grad - delta)).astype(BF)
+            value_part = nn_dot(probs.astype(BF), grad)
+            key_part = nn_dot(score_grad, query)
+            if at == 3:
+                dv[...] = value_part
+                dk[...] = key_part
+            else:
+                dv[:extent, :] += value_part
+                dk[:extent, :] += key_part
+            result = tn_dot(qkv_ref[:extent, 128:256], score_grad)
+            result = jnp.concatenate([result[:64, :part], result[64:, part:]], axis=0)
+            out_ref[rows, :128] = (result.T * 0.125).astype(BF)
+        out_ref[:, 128:256] = dk[...].astype(BF)
+        out_ref[:, 256:] = dv[...].astype(BF)
+        sums_ref[...] = jnp.zeros_like(sums_ref)
+        sums_ref[0:1, :] = jnp.sum(out_ref[:, :128].astype(F32), axis=0, keepdims=True)
+        sums_ref[1:2, :] = jnp.sum(out_ref[:, 256:].astype(F32), axis=0, keepdims=True)
+
+    return call(
+        LIGHT,
+        kernel,
+        (pairs,),
+        [tile((length, 384), lambda i, info: (0, i))]
+        + [tile((half_rows, 128), lambda i, info: (0, pair + i))] * 2
+        + [tile((8, length), lambda i, info: (i, 0))],
+        [
+            (tile((length, 384), lambda i, info: (0, i)), (length, 384 * pairs), BF),
+            (tile((8, 128), lambda i, info: (i, 0)), (8 * pairs, 128), F32),
+        ],
+        [pltpu.VMEM((length, 128), BF), pltpu.VMEM((length, 128), F32), pltpu.VMEM((length, 128), F32)],
+        (info, qkv, own_grad, peer_grad, lse),
+    )
+
+
+TAIL = (
+    0.11967499392384373,
+    0.1200623431946099,
+    0.10393185617157874,
+    0.11668075888774873,
+    -0.03403495598672794,
+    0.18794905931773562,
+    -0.1480832678227233,
+    0.03381921655662456,
+)
+
+
+def gelu_both(inner):
+    scale = 1.0 / (1.0 + 0.3 * jnp.abs(inner))
+    bell = jnp.exp2(inner * inner * (-0.5 * LOG2E))
+    tail = TAIL[-1]
+    for term in TAIL[-2::-1]:
+        tail = tail * scale + term
+    tail = tail * scale * bell
+    below = jnp.where(inner < 0, tail, 1.0 - tail)
+    return inner * below, below + (inner * 0.3989422804014327) * bell
+
+
+def up_call(info, hidden, up_bias, up_pieces, start, carried):
+    first = start is not None
+    size = 768
+    steps = hidden // 2 // size
+    skip = 0 if first else steps
+    count = len(up_pieces)
+    piece_rows = up_pieces[0].shape[0] // 4
+    if first:
+        own, step, mixed_own, mixed_peer, vectors = start
+        rows, width = own.shape
+        parts = len(mixed_own)
+        args = [own, step, *mixed_own, *mixed_peer, vectors, *up_pieces]
+        specs = [fixed(arg.shape) for arg in args[: 3 + 2 * parts]]
+        specs += [fixed((4 * piece_rows, width)) for _ in up_pieces]
+        aliases = {}
+    else:
+        args = list(carried)
+        rows, width = args[0].shape
+        specs = [fixed(args[0].shape)] + [pl.BlockSpec(memory_space=pl.ANY)] * 2
+        aliases = {3 + count + at: at for at in range(2)}
+    half = width // 2
+
+    def kernel(info, ub_ref, *rest):
+        up_refs, rest = rest[:count], rest[count:]
+        if first:
+            own_ref, step_ref = rest[:2]
+            mo_refs, mp_refs = rest[2 : 2 + parts], rest[2 + parts : 2 + 2 * parts]
+            vec_ref = rest[2 + 2 * parts]
+            out_refs, rest = rest[3 + 2 * parts : 3 + 2 * parts + count], rest[3 + 2 * parts + count :]
+            act_ref, slope_ref, norm_ref, root_ref, low_ref, up_weight, out_weight, total = rest
+
+            @pl.when(pl.program_id(0) == 0)
+            def _():
+                put_rows(info, out_refs, out_weight, piece_rows)
+                here = pl.multiple_of(info[CTX] * half, half)
+                there = pl.multiple_of((1 - info[CTX]) * half, half)
+                mixed = jnp.concatenate([ref[...] for ref in mo_refs], axis=1)
+                total[...] = nn_dot(mixed, out_weight[pl.ds(here, half), :])
+                mixed = jnp.concatenate([ref[...] for ref in mp_refs], axis=1)
+                total[...] += nn_dot(mixed, out_weight[pl.ds(there, half), :])
+
+                def body(at, carry):
+                    entries = own_ref[at, :].astype(F32) + step_ref[...].astype(F32)
+                    entries = entries + (total[at, :] + row(vec_ref, BIAS_O))
+                    center = entries - mean_last(entries)
+                    root = lax.rsqrt(mean_last(center * center) + norm_epsilon)
+                    norm = center * root
+                    norm_ref[at, :] = norm
+                    root_ref[at, :] = jnp.broadcast_to(root, (NORM, 128))
+                    low_ref[at, :] = (norm * row(vec_ref, GAIN_1) + row(vec_ref, SHIFT_1)).astype(BF)
+                    return carry
+
+                by_rows(rows, body, NORM)(0)
+        else:
+            low_ref, _, _, act_ref, slope_ref, up_weight = rest
+
+        put_rows(info, up_refs, up_weight, piece_rows)
+
+        for start in range(0, rows, 128):
+            places = slice(start, start + 128)
+            act, slope = gelu_both(nn_dot(low_ref[places, :], up_weight[...]) + ub_ref[...])
+            act_ref[places, :] = act.astype(BF)
+            slope_ref[places, :] = slope.astype(BF)
+
+    outs = [(tile((rows, size), lambda i, info: (0, skip + i)), (rows, hidden), BF)] * 2
+    scratch = [pltpu.VMEM((width, size), BF)]
+    if first:
+        outs += [
+            (fixed((rows, width)), (rows, width), F32),
+            (fixed((rows, 128)), (rows, 128), F32),
+            (fixed((rows, width)), (rows, width), BF),
+        ]
+        scratch += [pltpu.VMEM((width, width), BF), pltpu.VMEM((rows, width), F32)]
+    at_column = 1 if first else 0
+    return call(
+        LIGHT,
+        kernel,
+        (steps,),
+        [tile((1, size), lambda i, info: (0, skip + i))]
+        + [tile((4 * piece_rows, size), lambda i, info: (0, at_column + i)) for _ in up_pieces]
+        + specs,
+        outs,
+        scratch,
+        (info, up_bias, *up_pieces, *args),
+        aliases,
+    )
+
+
+def down_call(info, act, norm_one, cotangent, vectors, pieces):
+    rows, hidden = act.shape
+    width = cotangent.shape[1]
+    size, part, run = 256, 128, hidden // 8
+    products, norms, grads = width // size, rows // part, 8
+    count = len(pieces)
+    piece_rows = pieces[0].shape[0] // 4
+
+    def norm_at(i, info):
+        return (jnp.clip(i - products, 0, norms - 1), 0)
+
+    def place_at(i, info):
+        return (info[PLACES + jnp.maximum(i - products - norms, 0)], 0)
+
+    def kernel(info, act_ref, norm_ref, cot_ref, vec_ref, *rest):
+        refs, rest = rest[:count], rest[count:]
+        res_ref, dz_ref, df_ref, sums_ref, keep_ref, send_ref, weight, feed, both = rest
+        at = pl.program_id(0)
+
+        @pl.when(at < products)
+        def _():
+            put_rows(info, refs, weight, piece_rows, DOWN)
+            feed[at] = nn_dot(act_ref[...], weight[...])
+
+        @pl.when(at == 0)
+        def _():
+            sums_ref[...] = jnp.zeros_like(sums_ref)
+
+        @pl.when(jnp.logical_and(at >= products, at < products + norms))
+        def _():
+            def body(rows_here, carry):
+                bias_sum, gain_sum, shift_sum = carry
+                places = pl.ds(pl.multiple_of((at - products) * part + rows_here.start, NORM), NORM)
+                entries = jnp.concatenate([feed[step, places, :] for step in range(products)], axis=-1)
+                entries = entries + row(vec_ref, BIAS_D)
+                entries = entries + (norm_ref[rows_here, :] * row(vec_ref, GAIN_1) + row(vec_ref, SHIFT_1))
+                center = entries - mean_last(entries)
+                root = lax.rsqrt(mean_last(center * center) + norm_epsilon)
+                norm = center * root
+                res_ref[rows_here, :] = norm * row(vec_ref, GAIN_2) + row(vec_ref, SHIFT_2)
+                cot = cot_ref[rows_here, :].astype(F32)
+                scaled = cot * row(vec_ref, GAIN_2)
+                dz = root * (scaled - mean_last(scaled) - norm * mean_last(scaled * norm))
+                dz_ref[rows_here, :] = dz
+                low = dz.astype(BF)
+                df_ref[places, :] = low
+                return (
+                    bias_sum + fold(low.astype(F32)),
+                    gain_sum + fold(cot * norm),
+                    shift_sum + fold(cot),
+                )
+
+            zero = jnp.zeros((8, width), F32)
+            sums = by_rows(part, body, NORM)((zero, zero, zero))
+            for step in range(3):
+                sums_ref[step : step + 1, :] += jnp.sum(sums[step], axis=0, keepdims=True)
+
+        @pl.when(at >= products + norms)
+        def _():
+            lanes = pl.ds(pl.multiple_of((at - products - norms) * run, run), run)
+            both[...] = tn_dot(act_ref[:, lanes], df_ref[...]).astype(BF)
+            core = info[CORE]
+            keep_ref[...] = both[pl.ds(pl.multiple_of(core * piece_rows, 16), piece_rows), :]
+            send_ref[...] = both[pl.ds(pl.multiple_of((1 - core) * piece_rows, 16), piece_rows), :]
+
+    return call(
+        LIGHT,
+        kernel,
+        (products + norms + grads,),
+        [
+            fixed((rows, hidden)),
+            tile((part, width), norm_at),
+            tile((part, width), norm_at),
+            fixed(vectors.shape),
+        ]
+        + [tile((4 * piece_rows, size), lambda i, info: (0, jnp.minimum(i, products - 1))) for _ in pieces],
+        [
+            (tile((part, width), norm_at), (rows, width), F32),
+            (tile((part, width), norm_at), (rows, width), F32),
+            (fixed((rows, width)), (rows, width), BF),
+            (fixed((8, width)), (8, width), F32),
+            (tile((piece_rows, width), place_at), (hidden // 2, width), BF),
+            (tile((piece_rows, width), place_at), (hidden // 2, width), BF),
+        ],
+        [
+            pltpu.VMEM((hidden, size), BF),
+            pltpu.VMEM((products, rows, size), F32),
+            pltpu.VMEM((run, width), BF),
+        ],
+        (info, act, norm_one, cotangent, vectors, *pieces),
+    )
+
+
+def layer_grad_call(
+    info, feed_grad, slope, low_one, second_in, norm_one, root_one, vectors, mixed_own, mixed_peer, down, first, second
+):
+    rows, width = feed_grad.shape
+    hidden = slope.shape[1]
+    steps = hidden // width
+    count = len(down)
+    down_rows, up_rows = down[0].shape[0] // 4, first[0].shape[0] // 4
+    half = width // 2
+    pairs = len(mixed_own)
+
+    def kernel(info, df_ref, slope_ref, low_ref, dz_ref, norm_ref, root_ref, vec_ref, *rest):
+        mixed_refs, rest = rest[: 2 * pairs], rest[2 * pairs :]
+        down_refs, first_refs, second_refs, out_refs = (rest[count * at : count * at + count] for at in range(4))
+        rest = rest[4 * count :]
+        keep_ref, send_ref, bias_ref, dz1_ref, own_ref, peer_ref, sums_ref = rest[:7]
+        down_weight, up_weight, total, both, da = rest[7:]
+        at = pl.program_id(0)
+
+        @pl.when(at == 0)
+        def _():
+            total[...] = dz_ref[...]
+
+        here_z = info[ZS + jnp.minimum(at, steps - 1)]
+
+        @pl.when(jnp.logical_and(here_z < steps // 2, at < steps))
+        def _():
+            put_rows(info, first_refs, up_weight, up_rows)
+
+        @pl.when(jnp.logical_and(here_z >= steps // 2, at < steps))
+        def _():
+            put_rows(info, second_refs, up_weight, up_rows)
+
+        for far in range(2):
+
+            @pl.when(jnp.logical_and(at >= far * 2, at < far * 2 + 2))
+            def _():
+                for core in range(2):
+                    piece = down_refs[2 * core + far]
+                    for step in range(2):
+                        place = pl.multiple_of(info[DOWN + 8 * core + step] % 4 * down_rows, 16)
+                        down_weight[pl.ds(place, down_rows), :] = piece[step * down_rows : (step + 1) * down_rows, :]
+
+        @pl.when(at < steps)
+        def _():
+            inner = (nt_dot(df_ref[...], down_weight[...]) * slope_ref[...].astype(F32)).astype(BF)
+            bias_ref[...] = jnp.sum(inner.astype(F32), axis=0, keepdims=True)
+            both[...] = tn_dot(low_ref[...], inner).astype(BF)
+            total[...] += nt_dot(inner, up_weight[...])
+
+        @pl.when(at == steps - 1)
+        def _():
+            put_rows(info, out_refs, up_weight, up_rows)
+
+            def body(at, carry):
+                gain_sum, shift_sum, bias_sum = carry
+                grad = total[at, :]
+                norm = norm_ref[at, :]
+                scaled = grad * row(vec_ref, GAIN_1)
+                dz = root_ref[at, 0:1] * (scaled - mean_last(scaled) - norm * mean_last(scaled * norm))
+                dz1_ref[at, :] = dz
+                low = dz.astype(BF)
+                da[at, :] = low
+                return gain_sum + fold(grad * norm), shift_sum + fold(grad), bias_sum + fold(low.astype(F32))
+
+            zero = jnp.zeros((8, width), F32)
+            gain_sum, shift_sum, bias_sum = by_rows(rows, body, NORM)((zero, zero, zero))
+            sums_ref[...] = jnp.zeros_like(sums_ref)
+            sums_ref[0:1, :] = jnp.sum(bias_sum, axis=0, keepdims=True)
+            sums_ref[1:2, :] = jnp.sum(gain_sum, axis=0, keepdims=True)
+            sums_ref[2:3, :] = jnp.sum(shift_sum, axis=0, keepdims=True)
+            here = pl.multiple_of(info[CTX] * half, half)
+            there = pl.multiple_of((1 - info[CTX]) * half, half)
+            own_ref[...] = nt_dot(da[...], up_weight[pl.ds(here, half), :]).astype(BF)
+            peer_ref[...] = nt_dot(da[...], up_weight[pl.ds(there, half), :]).astype(BF)
+
+        @pl.when(at == steps)
+        def _():
+            for side, start in ((0, info[CTX] * half), (1, (1 - info[CTX]) * half)):
+                mixed = jnp.concatenate([ref[...] for ref in mixed_refs[side * pairs : (side + 1) * pairs]], axis=1)
+                both[pl.ds(pl.multiple_of(start, half), half), :] = tn_dot(mixed, da[...]).astype(BF)
+
+        permute_rows(info, BLOCKS, both, keep_ref, send_ref, slice(None), up_rows)
+
+    def step_at(i, info):
+        return (0, info[ZS + jnp.minimum(i, steps - 1)])
+
+    def first_at(i, info):
+        return (0, 1 + jnp.minimum(info[ZS + jnp.minimum(i, steps - 1)], 1))
+
+    def second_at(i, info):
+        return (0, jnp.maximum(info[ZS + jnp.minimum(i, steps - 1)] - 2, 0))
+
+    def grads_at(i, info):
+        return (0, jnp.where(i < steps, info[ZS + jnp.minimum(i, steps - 1)], steps))
+
+    columns = hidden + width
+    return call(
+        LIGHT,
+        kernel,
+        (steps + 1,),
+        [
+            fixed((rows, width)),
+            tile((rows, width), step_at),
+            fixed((rows, width)),
+            fixed((rows, width)),
+            fixed((rows, width)),
+            fixed((rows, 128)),
+            fixed(vectors.shape),
+        ]
+        + [fixed(array.shape) for array in (*mixed_own, *mixed_peer)]
+        + [
+            tile((2 * down_rows, width), lambda i, info, far=far: (jnp.clip(i - 2 * far, 0, 1), 0))
+            for _ in range(2)
+            for far in range(2)
+        ]
+        + [tile((4 * up_rows, width), first_at) for _ in first]
+        + [tile((4 * up_rows, width), second_at) for _ in second]
+        + [fixed((4 * up_rows, width)) for _ in first],
+        [
+            (tile((half, width), grads_at), (half, columns), BF),
+            (tile((half, width), grads_at), (half, columns), BF),
+            (tile((1, width), step_at), (1, hidden), F32),
+            (fixed((rows, width)), (rows, width), F32),
+            (fixed((rows, half)), (rows, half), BF),
+            (fixed((rows, half)), (rows, half), BF),
+            (fixed((8, width)), (8, width), F32),
+        ],
+        [
+            pltpu.VMEM((width, width), BF),
+            pltpu.VMEM((width, width), BF),
+            pltpu.VMEM((rows, width), F32),
+            pltpu.VMEM((width, width), BF),
+            pltpu.VMEM((rows, width), BF),
+        ],
+        (
+            info,
+            feed_grad,
+            slope,
+            low_one,
+            second_in,
+            norm_one,
+            root_one,
+            vectors,
+            *mixed_own,
+            *mixed_peer,
+            *down,
+            *first,
+            *second,
+            *first,
+        ),
+    )
+
+
+def early_call(info, low_zero, grads, pieces):
+    length, width = low_zero.shape
+    pairs = grads.shape[1] // 384
+    half = width // 2
+    rows = width // 16
+    count = len(pieces)
+
+    def kernel(info, low_ref, grad_ref, *rest):
+        refs, (keep_ref, send_ref, out_ref, weight, both) = rest[:count], rest[count:]
+        at = pl.program_id(0)
+        put_rows(info, refs, weight, rows)
+        both[...] = tn_dot(low_ref[...], grad_ref[...]).astype(BF)
+
+        @pl.when(at == 0)
+        def _():
+            out_ref[...] = nt_dot(grad_ref[...], weight[...])
+
+        @pl.when(at > 0)
+        def _():
+            out_ref[...] += nt_dot(grad_ref[...], weight[...])
+
+        permute_rows(info, BLOCKS, both, keep_ref, send_ref, slice(None), rows)
+
+    return call(
+        LIGHT,
+        kernel,
+        (pairs,),
+        [fixed((length, width)), tile((length, 384), lambda i, info: (0, i))]
+        + [tile((4 * rows, 384), lambda i, info: (0, i)) for _ in pieces],
+        [
+            (tile((half, 384), lambda i, info: (0, i)), (half, 384 * pairs), BF),
+            (tile((half, 384), lambda i, info: (0, i)), (half, 384 * pairs), BF),
+            (fixed((length, width)), (length, width), F32),
+        ],
+        [pltpu.VMEM((width, 384), BF), pltpu.VMEM((width, 384), BF)],
+        (info, low_zero, grads, *pieces),
+    )
+
+
+def late_call(info, low_zero, grads, partial, first_in, pieces, pair, sums):
+    length, width = low_zero.shape
+    half = width // 2
+    rows = width // 16
+    count = len(pieces)
+    parts = len(sums) - 3
+
+    def kernel(info, low_ref, grad_ref, partial_ref, in_ref, *rest):
+        refs, sum_refs, rest = rest[:count], rest[count : count + parts + 3], rest[count + parts + 3 :]
+        keep_ref, send_ref, peer_ref, own_ref, weight, both, stacked, columns = rest
+        at = pl.program_id(0)
+
+        @pl.when(at == 0)
+        def _():
+            put_rows(info, refs, weight, rows)
+            both[...] = tn_dot(low_ref[...], grad_ref[...]).astype(BF)
+            permute_rows(info, BLOCKS, both, keep_ref, send_ref, slice(0, 384), rows)
+            stacked[...] = jnp.zeros_like(stacked)
+            step = 0
+            for ref in sum_refs[:parts]:
+                for start in range(0, ref.shape[0], 8):
+                    lanes = pl.ds(pl.multiple_of(info[CTX] * half + 128 * step, 128), 128)
+                    stacked[0:8, lanes] = ref[start : start + 8, :]
+                    step += 1
+            for step in range(3):
+                stacked[8 + 8 * step : 16 + 8 * step, :] = sum_refs[parts + step][...]
+            columns[...] = stacked[...].T.astype(BF)
+            permute_rows(info, BLOCKS, columns, keep_ref, send_ref, slice(384, 512), rows)
+
+        slot = jnp.where(at < 2, at + 2, at - 2)
+        places = pl.ds(pl.multiple_of(info[IDS + slot] * BLOCK, BLOCK), BLOCK)
+        result = partial_ref[...] + nt_dot(grad_ref[places, :], weight[...])
+
+        @pl.when(at < 2)
+        def _():
+            peer_ref[...] = result.astype(BF)
+
+        @pl.when(at >= 2)
+        def _():
+            own_ref[...] = result + in_ref[...]
+
+    def slot_at(i, info):
+        return (info[IDS + jnp.where(i < 2, i + 2, i - 2)], 0)
+
+    def own_at(i, info):
+        return (jnp.maximum(i - 2, 0), 0)
+
+    return call(
+        LIGHT,
+        kernel,
+        (4,),
+        [
+            fixed((length, width)),
+            fixed((length, 384)),
+            tile((BLOCK, width), slot_at),
+            tile((BLOCK, width), own_at),
+        ]
+        + [pl.BlockSpec((4 * rows, 384), lambda i, info: (0, pair), pipeline_mode=pl.Buffered(1)) for _ in pieces]
+        + [fixed(array.shape) for array in sums],
+        [
+            (fixed((half, 512)), (half, 512), BF),
+            (fixed((half, 512)), (half, 512), BF),
+            (tile((BLOCK, width), lambda i, info: (jnp.minimum(i, 1), 0)), (length // 2, width), BF),
+            (tile((BLOCK, width), own_at), (length // 2, width), F32),
+        ],
+        [
+            pltpu.VMEM((width, 384), BF),
+            pltpu.VMEM((width, 384), BF),
+            pltpu.VMEM((128, width), F32),
+            pltpu.VMEM((width, 128), BF),
+        ],
+        (info, low_zero, grads, partial, first_in, *pieces, *sums),
+    )
+
+
+def split_heads_shards(
+    ring,
+    tokens,
+    step_embed,
+    block_ids,
+    cotangent,
+    project_weight,
+    project_bias,
+    output_weight,
+    output_bias,
+    first_gain,
+    first_shift,
+    up_weight,
+    up_bias,
+    down_weight,
+    down_bias,
+    second_gain,
+    second_shift,
+):
+    rows, width = tokens.shape[1:]
+    half = width // 2
+    hidden = up_weight.shape[1]
+    spot = lax.axis_index("fsdp")
+    ctx = lax.axis_index("ctx")
+    core = spot % 2
+
+    def flip(array, bit):
+        return lax.ppermute(array, "fsdp", [(at, at ^ bit) for at in range(ring)])
+
+    def ctx_flip(array):
+        return lax.ppermute(array, "ctx", [(0, 1), (1, 0)])
+
+    def join(array, other):
+        return jnp.concatenate([array, other], axis=0)
+
+    def after(values, done):
+        return lax.optimization_barrier((values, done))[0]
+
+    def spots(*bits):
+        return [spot ^ sum(bit for step, bit in enumerate(bits) if at >> step & 1) for at in range(ring)]
+
+    NEXT, OVER, SIDE = 4, 8, 2
+    tokens_own = tokens.reshape(rows, width)
+    tokens_peer = ctx_flip(tokens_own)
+    ids_peer = ctx_flip(block_ids)
+    ids = jnp.concatenate([block_ids, ids_peer], axis=1).reshape(4)
+    order = jnp.arange(4, dtype=jnp.int32)
+    slots = jnp.sum(jnp.where(ids[None, :] == order[:, None], order[None, :], 0), axis=1)
+    z_at, x_at = spot // 4, spot // 2 % 2
+    places_of = [(z_at ^ z) % 2 * 4 + (z_at ^ z) // 2 * 2 + (x_at ^ x) for z in range(4) for x in range(2)]
+    down_zs = [z_at ^ z for z in (0, 2, 1, 3)]
+    info = jnp.concatenate(
+        [
+            jnp.stack(spots(OVER, NEXT, SIDE, 1) + spots(OVER, NEXT, SIDE, 1)).astype(jnp.int32),
+            ids,
+            slots,
+            jnp.stack([ctx, core] + spots(SIDE, OVER, NEXT, 1) + places_of + down_zs).astype(jnp.int32),
+        ]
+    )
+
+    pairs = half // 128
+    share = width // ring
+    hidden_share = hidden // ring
+    plane = lax.dynamic_slice_in_dim(project_weight.reshape(share, 3, width), ctx * half, half, 2)
+    plane = jnp.transpose(plane.reshape(share, 3, pairs, 128), (0, 2, 1, 3)).reshape(share, 3 * half)
+    small = [
+        project_bias,
+        output_bias[None],
+        first_gain[None],
+        first_shift[None],
+        down_bias[None],
+        second_gain[None],
+        second_shift[None],
+        up_bias.reshape(4, share),
+    ]
+    small = jnp.concatenate(small, axis=0)
+    small = jnp.pad(small, ((0, 128 - small.shape[0]), (0, 0))).T
+    project_share = jnp.concatenate([plane, small], axis=1).astype(BF)
+    first_share = jnp.concatenate([output_weight, up_weight[:, : hidden // 2]], axis=1).astype(BF)
+    second_share = up_weight[:, hidden // 2 :].astype(BF)
+    down_share = down_weight.astype(BF)
+
+    project_2 = join(project_share, flip(project_share, OVER))
+    down_2 = join(down_share, flip(down_share, SIDE))
+    project_4 = join(project_2, flip(project_2, NEXT))
+    first_share = after(first_share, project_2)
+    first_2 = join(first_share, flip(first_share, OVER))
+    project_x = flip(project_4, SIDE)
+    second_share = after(second_share, first_2)
+    second_got = flip(second_share, OVER)
+    first_2 = after(first_2, project_4)
+    first_4 = join(first_2, flip(first_2, NEXT))
+    project_pieces = [project_4, project_x, *[flip(piece, 1) for piece in (project_4, project_x)]]
+
+    first_x = flip(first_4, SIDE)
+    second_2 = after(join(second_share, second_got), first_4)
+    second_got = flip(second_2, NEXT)
+    down_2 = after(down_2, second_2)
+    down_got = flip(down_2, OVER)
+    qkv_early, mixed_early, mixed_send, lse_early, low_zero, vectors = attend_call(
+        info,
+        0,
+        pairs - 1,
+        [after(tokens_own, (first_4, second_2, down_2)), tokens_peer, step_embed],
+        project_pieces,
+        None,
+    )
+    peer_early = ctx_flip(mixed_send)
+    up_bias_all = jnp.transpose(vectors[BIAS_U : BIAS_U + 4].reshape(4, ring, share), (1, 0, 2)).reshape(1, hidden)
+    second_4 = join(second_2, after(second_got, mixed_send))
+    qkv_late, mixed_late, out, lse_late = attend_call(
+        info, pairs - 1, 1, [after(low_zero, second_4)], project_pieces, vectors
+    )
+    mixed_own = [mixed_early, mixed_late]
+    mixed_peer = [peer_early, ctx_flip(out)]
+    first_x = after(first_x, (out, peer_early))
+    second_x = flip(after(second_4, first_x), SIDE)
+    down_4 = join(down_2, after(down_got, out))
+    down_x = flip(down_4, NEXT)
+    first_pieces = [first_4, first_x, *[flip(piece, 1) for piece in (after(first_4, out), first_x)]]
+    start = [after(tokens_own, down_4), step_embed, mixed_own, mixed_peer, vectors]
+    act, slope, norm_one, root_one, low_one = up_call(info, hidden, up_bias_all, first_pieces, start, None)
+    second_pieces = [second_4, second_x, *[flip(piece, 1) for piece in after((second_4, second_x), low_one)]]
+    low_next = after(low_one, second_pieces)
+    act, slope = up_call(info, hidden, up_bias_all, second_pieces, None, (low_next, act, slope))
+    down_pieces = [down_4, down_x, *[flip(piece, 1) for piece in after((down_4, down_x), act)]]
+    result, second_in, feed_grad, second_sums, down_keep, down_send = down_call(
+        info, act, norm_one, cotangent.reshape(rows, width), vectors, down_pieces
+    )
+
+    def add(left, right):
+        return (left.astype(F32) + right.astype(F32)).astype(BF)
+
+    def halves(array):
+        middle = array.shape[0] // 2
+        return array[:middle], array[middle:]
+
+    def add_halves(left, right):
+        return [add(*both) for both in zip(halves(left), halves(right))]
+
+    def finish(total):
+        return total.astype(F32) + ctx_flip(total).astype(F32)
+
+    down_near, down_far = add_halves(down_keep, flip(down_send, 1))
+    feed_next = after(feed_grad, (down_far, down_near))
+    down_got = flip(down_far, NEXT)
+    layer_keep, layer_send, up_bias_sums, first_in, grad_own, grad_peer, first_sums = layer_grad_call(
+        info,
+        feed_next,
+        slope,
+        low_one,
+        second_in,
+        norm_one,
+        root_one,
+        vectors,
+        mixed_own,
+        mixed_peer,
+        down_pieces,
+        first_pieces,
+        second_pieces,
+    )
+    grad_recv = ctx_flip(grad_peer)
+    down_got = after(down_got, layer_keep)
+    layer_got = flip(after(layer_send, down_got), 1)
+    up_sums = jnp.transpose(up_bias_sums.reshape(ring, 4, share), (1, 0, 2)).reshape(4, width)
+    up_sums = jnp.pad(up_sums, ((0, 4), (0, 0)))
+    layer_near, layer_far = add_halves(layer_keep, layer_got)
+    near_first, near_last = halves(layer_near)
+    far_first, far_last = halves(layer_far)
+    layer_got_last = flip(far_last, SIDE)
+    layer_got_first = flip(far_first, SIDE)
+    down_near, down_far = add_halves(down_near, down_got)
+    down_got = flip(down_far, OVER)
+    grad_own = after(grad_own, (layer_far, layer_near, down_far))
+    grads_early, sums_early = attend_back_call(info, 0, qkv_early, grad_own, grad_recv, lse_early)
+    layer_out = add(near_last, after(layer_got_last, grads_early))
+    layer_got_last = flip(layer_out, NEXT)
+    down_near, down_far = add_halves(down_near, after(down_got, grads_early))
+    down_got = flip(down_far, SIDE)
+    grad_own = after(grad_own, (layer_out, down_far, down_near))
+    grads_late, sums_late = attend_back_call(info, pairs - 1, qkv_late, grad_own, grad_recv, lse_late)
+    early_keep, early_send, partial = early_call(info, low_zero, after(grads_early, grads_late), project_pieces)
+    early_got = flip(early_send, 1)
+    layer_near, layer_far = halves(
+        after(near_first, early_send).astype(F32) + layer_got_first.astype(F32) + layer_got_last.astype(F32)
+    )
+    layer_far = layer_far.astype(BF)
+    layer_got = flip(layer_far, OVER)
+    down_total = add(down_near, after(down_got, early_send))
+    grad_down_weight = finish(down_total)
+    late_keep, late_send, peer_part, own_part = late_call(
+        info,
+        low_zero,
+        after(grads_late, (layer_far, layer_near, down_total)),
+        partial,
+        first_in,
+        project_pieces,
+        pairs - 1,
+        [sums_early, sums_late, first_sums, second_sums, up_sums],
+    )
+    other_part = ctx_flip(peer_part)
+    early_near, early_far = add_halves(early_keep, after(early_got, late_keep))
+    early_got = flip(early_far, SIDE)
+    layer_got = after(layer_got, late_keep)
+    late_near, late_far = add_halves(late_keep, flip(after(late_send, layer_got), 1))
+    late_got = flip(late_far, SIDE)
+    layer_total = add(layer_near, layer_got)
+    early_near, early_far = add_halves(early_near, early_got)
+    late_near, late_far = add_halves(late_near, late_got)
+    project_near = jnp.concatenate([early_near, late_near], axis=1)
+    project_far = jnp.concatenate([early_far, late_far], axis=1)
+    project_near, project_far = add_halves(project_near, flip(project_far, NEXT))
+    project_half = add(project_near, flip(project_far, OVER))
+    token_grad = own_part + other_part.astype(F32)
+
+    layer_sum = finish(layer_total)
+    project_other = ctx_flip(project_half)
+
+    def by_kind(array):
+        array = array[:, : 3 * half].reshape(share, pairs, 3, 128)
+        return jnp.transpose(array, (0, 2, 1, 3)).reshape(share, 3, 1, half)
+
+    mine, other = by_kind(project_half), by_kind(project_other)
+    first = ctx == 0
+    grad_project_weight = (
+        jnp.concatenate([jnp.where(first, mine, other), jnp.where(first, other, mine)], axis=2)
+        .reshape(share, 3 * width)
+        .astype(F32)
+    )
+    columns = (project_half[:, 3 * half :].astype(F32) + project_other[:, 3 * half :].astype(F32)).T
+
+    return (
+        result.reshape(1, rows, width),
+        token_grad.reshape(1, rows, width),
+        grad_project_weight,
+        columns[:2],
+        layer_sum[:, hidden : hidden + width],
+        columns[8],
+        columns[9],
+        columns[10],
+        layer_sum[:, :hidden],
+        columns[24:28].reshape(hidden_share),
+        grad_down_weight,
+        columns[16],
+        columns[17],
+        columns[18],
+    )
+
+
 def solution(mesh):
+    ring = mesh.shape["fsdp"]
+    body = shards
+    if mesh.shape["ctx"] == 2 and ring % 8 == 0 and ring == 16:
+        body = functools.partial(split_heads_shards, ring)
     return jax.shard_map(
-        shards,
+        body,
         mesh=mesh,
         in_specs=(
             P("fsdp", "ctx", None),

time: 863 us -> 294 us (0.34)
  waiting for transfers between devices: 419 us -> 86.6 us
  blocking collectives: 154 us -> 0 us
  matrix products: 150 us -> 0 us
  Pallas kernels: 0 us -> 112 us
  starting transfers between devices: 0.83 us -> 44.4 us
  local copies, waits for them, and re-layouts: 63.7 us -> 25.8 us
  other arithmetic: 42.3 us -> 20 us
  between operations: 18.2 us -> 1.75 us
  loops' own time: 8.8 us -> 0 us
    reduce_scatter x6 -> x0, waiting for transfers between devices: 253 us -> none  [the longest x1 79 us: shards(): lax.psum_scatter(grad_up_weight.astype(jnp.bfloat16), 'fsdp', scatter_dim...]
    dot_general x54 -> x0, matrix products: 150 us -> none  [the longest x4 35 us: product(): return jnp.dot(left, right, preferred_element_type=jnp.float32)]
    unnamed x3 -> x0, blocking collectives: 126 us -> none
    pallas_call x0 -> x10, Pallas kernels: none -> 112 us  [call(): pl.pallas_call(kernel, grid_spec=pltpu.PrefetchScalarGridSpec(num_scalar_...]
    all_gather x6 -> x0, waiting for transfers between devices: 87.2 us -> none  [the longest x1 33.6 us: shards(): lax.all_gather(down_weight.astype(jnp.bfloat16), 'fsdp', axis=0, tiled=True)]
    ppermute x0 -> x44, waiting for transfers between devices: none -> 86.6 us  [the longest x35 65.6 us: flip(): return lax.ppermute(array, 'fsdp', [(at, at ^ bit) for at in range(ring)])]
    unnamed x15 -> x0, waiting for transfers between devices: 50.7 us -> none
    ppermute x0 -> x44, starting transfers between devices: none -> 44.4 us  [the longest x35 35.9 us: flip(): return lax.ppermute(array, 'fsdp', [(at, at ^ bit) for at in range(ring)])]
  transfers between devices with their start and end apart: 14 -> 44, of which waited for: 10 -> 23; matrix products, arithmetic and copies ran while one was open for 13% -> 9% of each run, Pallas kernels for 0% -> 32%
where the time goes in v1:
time: 294 us; the launch traced here: 290 us
  Pallas kernels  112 us (38%)
  waiting for transfers between devices  86.6 us (29%)
  starting transfers between devices  44.4 us (15%)
  local copies, waits for them, and re-layouts  25.8 us (9%)
  other arithmetic  20 us (7%)
    pallas_call x10, Pallas kernels, call(): pl.pallas_call(kernel, grid_spec=pltpu.PrefetchScalarGridSpec(num_scalar_...  112 us
    ppermute x35, waiting for transfers between devices, flip(): return lax.ppermute(array, 'fsdp', [(at, at ^ bit) for at in range(ring)])  65.6 us
    ppermute x35, starting transfers between devices, flip(): return lax.ppermute(array, 'fsdp', [(at, at ^ bit) for at in range(ring)])  35.9 us
    ppermute x9, waiting for transfers between devices, ctx_flip(): return lax.ppermute(array, 'ctx', [(0, 1), (1, 0)])  20.9 us
    convert_element_type x13, other arithmetic, add(): return (left.astype(F32) + right.astype(F32)).astype(BF)  12.6 us
    unnamed x80, local copies, waits for them, and re-layouts  10.6 us
    ppermute x9, starting transfers between devices, ctx_flip(): return lax.ppermute(array, 'ctx', [(0, 1), (1, 0)])  8.46 us
  transfers between devices with their start and end apart: 44, of which 23 were waited for; matrix products, arithmetic and copies ran while one was open for 9% of the time, Pallas kernels for 32%

profile of v1, /device:TPU:0, one launch (start us, length us, event | category | flops | bytes accessed | tf_op | source)
XLA Modules:
  0.0 290.0 jit_solution(6083033771740890377)
XLA Ops:
  0.8 1.2 reshape.130
  2.7 4.1 %collective-permute-start.1 = (bf16[48,1280]{1,0:T(8,128)(2,1)S(1)}, bf16[48,1280]{1,0:T(8,128)(2,1)S(1)}, u32[]{:S(2)}, u32[]{:S(2)}) collective-permute-start(bf16[48,1280]{1,0:T(8,128)(2,1)S(1)} %pad_maximum_fusion.7), channel_id=1, source_target_pairs={{0,8},{1,9},{2,10},{3,11},{4,12},{5,13},{6,14},{7,15},{8,0},{9,1},... | collective-permute-start | bytes 368648 | tf_op jit(solution)/shard_map/ppermute | solution.py:1063
  6.9 1.6 collective-permute-start.6
  8.4 1.5 collective-permute-start
  10.8 1.2 collective-permute-done
  13.7 3.3 %collective-permute-start.2 = (bf16[48,2304]{1,0:T(8,128)(2,1)S(1)}, bf16[48,2304]{1,0:T(8,128)(2,1)S(1)}, u32[]{:S(2)}, u32[]{:S(2)}) collective-permute-start(bf16[48,2304]{1,0:T(8,128)(2,1)S(1)} %pad_maximum_fusion.5), channel_id=1, source_target_pairs={{0,8},{1,9},{2,10},{3,11},{4,12},{5,13},{6,14},{7,15},{8,0},{9,1},... | collective-permute-start | bytes 663560 | tf_op jit(solution)/shard_map/ppermute | solution.py:1063
  17.0 6.8 %collective-permute-done.2 = bf16[48,2304]{1,0:T(8,128)(2,1)S(1)} collective-permute-done((bf16[48,2304]{1,0:T(8,128)(2,1)S(1)}, bf16[48,2304]{1,0:T(8,128)(2,1)S(1)}, u32[]{:S(2)}, u32[]{:S(2)}) %collective-permute-start.2) | collective-permute-done | bytes 221216 | tf_op jit(solution)/shard_map/ppermute | solution.py:1063
  24.8 3.2 %collective-permute-start.4 = (bf16[96,2304]{1,0:T(8,128)(2,1)S(1)}, bf16[96,2304]{1,0:T(8,128)(2,1)S(1)}, u32[]{:S(2)}, u32[]{:S(2)}) collective-permute-start(bf16[96,2304]{1,0:T(8,128)(2,1)S(1)} %constant_dynamic-update-slice_fusion), channel_id=1, source_target_pairs={{0,4},{1,5},{2,6},{3,7},{4,0},{5,1},{6,2},{7,3},{8,12},{9,13},{10,... | collective-permute-start | bytes 1327112 | tf_op jit(solution)/shard_map/ppermute | solution.py:1063
  28.8 2.2 collective-permute-start.5
  31.0 1.5 collective-permute-start.8
  32.5 8.5 %collective-permute-done.4 = bf16[96,2304]{1,0:T(8,128)(2,1)S(1)} collective-permute-done((bf16[96,2304]{1,0:T(8,128)(2,1)S(1)}, bf16[96,2304]{1,0:T(8,128)(2,1)S(1)}, u32[]{:S(2)}, u32[]{:S(2)}) %collective-permute-start.4) | collective-permute-done | bytes 442400 | tf_op jit(solution)/shard_map/ppermute | solution.py:1063
  41.1 1.6 collective-permute-start.12
  43.6 1.6 collective-permute-start.11
  45.2 1.8 pad_maximum_fusion
  47.0 2.0 collective-permute-start.17
  49.1 1.7 constant_dynamic-update-slice_fusion.5
  52.4 11.4 %shard_map.263 = (bf16[1024,768]{1,0:T(8,128)(2,1)}, bf16[512,256]{1,0:T(8,128)(2,1)}, bf16[512,256]{1,0:T(8,128)(2,1)}, f32[16,1024]{1,0:T(8,128)}, bf16[1024,768]{1,0:T(8,128)(2,1)}, /*index=5*/f32[16,768]{1,0:T(8,128)}) custom-call(s32[70]{0:T(128)} %concatenate.53.info, bf16[512,768]{1,0:T(8,128)(2,1)} %bitcast.31.rest_0_.rest_4_, ...), custom_call_target="tpu_custom_call" | custom-call | flops 345000000 | bytes 1 | tf_op jit(solution)/shard_map/pallas_call | solution.py:354
  63.8 1.6 collective-permute-start.13
  65.4 1.7 constant_dynamic-update-slice_fusion.4.rest_0_.rest_12_
  67.1 6.5 %shard_map.264 = (bf16[1024,384]{1,0:T(8,128)(2,1)}, bf16[512,128]{1,0:T(8,128)(2,1)}, bf16[512,128]{1,0:T(8,128)(2,1)}, f32[8,1024]{1,0:T(8,128)}) custom-call(s32[70]{0:T(128)} %concatenate.53.info, bf16[1024,768]{1,0:T(8,128)(2,1)} %get-tuple-element.97.rest_0_.low_ref, bf16[192,1280]{1,0:T(8,128)(2,1)} %copy-done.1, bf16[192,1280]{1,0:T(8,128)(2,1)} %copy-done.4, ...), custom_call_target="tpu_custom_call" | custom-call | flops 345000000 | bytes 1 | tf_op jit(solution)/shard_map/pallas_call | solution.py:354
  74.3 1.9 constant_dynamic-update-slice_fusion.7
  76.9 1.9 constant_dynamic-update-slice_fusion.6.rest_0_.rest_4_
  81.9 2.7 collective-permute-done.18.rest_9_.rest_3_
  85.6 10.8 %shard_map.265 = (bf16[512,3072]{1,0:T(8,128)(2,1)}, bf16[512,3072]{1,0:T(8,128)(2,1)}, f32[512,768]{1,0:T(8,128)}, f32[512,128]{1,0:T(8,128)}, bf16[512,768]{1,0:T(8,128)(2,1)}) custom-call(s32[70]{0:T(128)} %concatenate.53.info, f32[1,3072]{1,0:T(1,128)} %reshape.135.ub_ref, bf16[192,2304]{1,0:T(8,128)(2,1)} %copy-done, bf16[192,2304]{1,0:T(8,128)(2,1)} %copy-done.2, ...), custom_call_target="tpu_custom_call" | custom-call | flops 345000000 | bytes 1 | tf_op jit(solution)/shard_map/pallas_call | solution.py:354
  97.0 1.7 collective-permute-done.19.rest_2_.rest_14_
  100.4 8.2 %shard_map.266 = (bf16[512,3072]{1,0:T(8,128)(2,1)}, bf16[512,3072]{1,0:T(8,128)(2,1)}) custom-call(s32[70]{0:T(128)} %concatenate.53.info, f32[1,3072]{1,0:T(1,128)} %reshape.135.ub_ref, bf16[192,1536]{1,0:T(8,128)(2,1)} %constant_dynamic-update-slice_fusion.4.rest_0_.rest_12_, ...), custom_call_target="tpu_custom_call", output_to_operand_aliasing={{0}: (7, {}), {1}: (8, {})} | custom-call | flops 345000000 | bytes 1 | tf_op jit(solution)/shard_map/pallas_call | solution.py:354
  109.2 2.5 collective-permute-done.22.rest_2_.rest_6_
  111.7 1.7 collective-permute-done.23.rest_3_.rest_7_
  113.4 1.1 copy-done.8
  114.5 17.6 %shard_map.267 = (f32[512,768]{1,0:T(8,128)}, f32[512,768]{1,0:T(8,128)}, bf16[512,768]{1,0:T(8,128)(2,1)}, f32[8,768]{1,0:T(8,128)}, bf16[1536,768]{1,0:T(8,128)(2,1)}, /*index=5*/bf16[1536,768]{1,0:T(8,128)(2,1)}) custom-call(s32[70]{0:T(128)} %concatenate.53.info, bf16[512,3072]{1,0:T(8,128)(2,1)} %get-tuple-element.112.act_ref, ...), custom_call_target="tpu_custom_call" | custom-call | flops 345000000 | bytes 1 | tf_op jit(solution)/shard_map/pallas_call | solution.py:354
  132.2 4.6 %collective-permute-done.24 = bf16[1536,768]{1,0:T(8,128)(2,1)S(1)} collective-permute-done((bf16[1536,768]{1,0:T(8,128)(2,1)}, bf16[1536,768]{1,0:T(8,128)(2,1)S(1)}, u32[]{:S(2)}, u32[]{:S(2)}) %collective-permute-start.24) | collective-permute-done | bytes 2359328 | tf_op jit(solution)/shard_map/ppermute | solution.py:1063
  136.9 2.2 add_convert_fusion.2
  139.0 1.3 collective-permute-start.25
  140.4 21.2 %shard_map.268 = (bf16[384,3840]{1,0:T(8,128)(2,1)}, bf16[384,3840]{1,0:T(8,128)(2,1)}, f32[1,3072]{1,0:T(1,128)}, f32[512,768]{1,0:T(8,128)}, bf16[512,384]{1,0...) custom-call(s32[70]{0:T(128)} %concatenate.53.info, bf16[512,768]{1,0:T(8,128)(2,1)} %get-tuple-element.121.df_ref, ...), custom_call_target="tpu_custom_call" | custom-call | flops 345000000 | bytes 1 | tf_op jit(solution)/shard_map/pallas_call | solution.py:354
  161.6 5.5 %collective-permute-done.25 = bf16[768,768]{1,0:T(8,128)(2,1)S(1)} collective-permute-done((bf16[768,768]{1,0:T(8,128)(2,1)S(1)}, bf16[768,768]{1,0:T(8,128)(2,1)S(1)}, u32[]{:S(2)}, u32[]{:S(2)}) %collective-permute-start.25) | collective-permute-done | bytes 1179680 | tf_op jit(solution)/shard_map/ppermute | solution.py:1063
  167.1 1.0 copy-done.13
  168.1 4.6 %collective-permute-done.26 = bf16[384,3840]{1,0:T(8,128)(2,1)S(1)} collective-permute-done((bf16[384,3840]{1,0:T(8,128)(2,1)}, bf16[384,3840]{1,0:T(8,128)(2,1)S(1)}, u32[]{:S(2)}, u32[]{:S(2)}) %collective-permute-start.26) | collective-permute-done | bytes 2949152 | tf_op jit(solution)/shard_map/ppermute | solution.py:1063
  172.7 2.6 add_convert_fusion
  175.3 1.2 fusion.1
  176.5 1.5 collective-permute-start.27
  179.0 1.1 add_convert_fusion.5
  180.1 2.5 collective-permute-start.29
  183.1 5.8 %collective-permute-done.28.peer_ref = bf16[512,384]{1,0:T(8,128)(2,1)S(1)} collective-permute-done((bf16[512,384]{1,0:T(8,128)(2,1)S(1)}, bf16[512,384]{1,0:T(8,128)(2,1)S(1)}, u32[]{:S(2)}, u32[]{:S(2)}) %collective-permute-start.28) | collective-permute-done | bytes 393248 | tf_op jit(solution)/shard_map/ppermute | solution.py:1066
  189.7 11.5 %shard_map.269 = (bf16[1024,768]{1,0:T(8,128)(2,1)}, f32[16,128]{1,0:T(8,128)}) custom-call(s32[70]{0:T(128)} %concatenate.53.info, bf16[1024,768]{1,0:T(8,128)(2,1)} %get-tuple-element.131.qkv_ref, bf16[512,384]{1,0:T(8,128)(2,1)} %get-tuple-element.137.own_ref, bf16[512,384]{1,0:T(8,128)(2,1)} %copy-done.12, f32[16,1024]{1,0:T(8,128)} %get-tuple-element.133.lse_ref), custom_call_target="tpu_custom_call" | custom-call | flops 345000000 | bytes 1 | tf_op jit(solution)/shard_map/pallas_call | solution.py:354
  201.2 2.1 add_convert_fusion.4
  203.3 1.2 collective-permute-start.31
  204.6 4.3 %collective-permute-done.29 = bf16[384,768]{1,0:T(8,128)(2,1)} collective-permute-done((bf16[384,768]{1,0:T(8,128)(2,1)}, bf16[384,768]{1,0:T(8,128)(2,1)}, u32[]{:S(2)}, u32[]{:S(2)}) %collective-permute-start.29) | collective-permute-done | bytes 589856 | tf_op jit(solution)/shard_map/ppermute | solution.py:1063
  208.9 1.9 add_convert_fusion.11
  211.3 6.9 %shard_map.270 = (bf16[1024,384]{1,0:T(8,128)(2,1)}, f32[8,128]{1,0:T(8,128)}) custom-call(s32[70]{0:T(128)} %concatenate.53.info, bf16[1024,384]{1,0:T(8,128)(2,1)} %get-tuple-element.117.qkv_ref, bf16[512,384]{1,0:T(8,128)(2,1)} %get-tuple-element.137.own_ref, bf16[512,384]{1,0:T(8,128)(2,1)} %copy-done.12, f32[8,1024]{1,0:T(8,128)} %get-tuple-element.138.lse_ref), custom_call_target="tpu_custom_call" | custom-call | flops 345000000 | bytes 1 | tf_op jit(solution)/shard_map/pallas_call | solution.py:354
  218.2 8.7 %shard_map.271 = (bf16[384,768]{1,0:T(8,128)(2,1)}, bf16[384,768]{1,0:T(8,128)(2,1)}, f32[1024,768]{1,0:T(8,128)}) custom-call(s32[70]{0:T(128)} %concatenate.53.info, bf16[1024,768]{1,0:T(8,128)(2,1)} %get-tuple-element.97.rest_0_.low_ref, bf16[1024,768]{1,0:T(8,128)(2,1)} %get-tuple-element.140.grad_ref, bf16[192,1280]{1,0:T(8,128)(2,1)} %copy-done.1, ...), custom_call_target="tpu_custom_call" | custom-call | flops 345000000 | bytes 1 | tf_op jit(solution)/shard_map/pallas_call | solution.py:354
  227.0 1.4 convert_add_fusion
  228.5 1.0 add_convert_fusion.10
  229.5 1.2 collective-permute-start.43
  232.7 8.8 %shard_map.272 = (bf16[384,512]{1,0:T(8,128)(2,1)}, bf16[384,512]{1,0:T(8,128)(2,1)}, bf16[512,768]{1,0:T(8,128)(2,1)}, f32[512,768]{1,0:T(8,128)}) custom-call(s32[70]{0:T(128)} %concatenate.53.info, bf16[1024,768]{1,0:T(8,128)(2,1)} %get-tuple-element.97.rest_0_.low_ref, bf16[1024,384]{1,0:T(8,128)(2,1)} %get-tuple-element.144.grad_ref, ...), custom_call_target="tpu_custom_call" | custom-call | flops 345000000 | bytes 1 | tf_op jit(solution)/shard_map/pallas_call | solution.py:354
  241.5 6.3 %collective-permute-done.36 = bf16[48,3840]{1,0:T(8,128)(2,1)S(1)} collective-permute-done((bf16[48,3840]{1,0:T(8,128)(2,1)S(1)}, bf16[48,3840]{1,0:T(8,128)(2,1)S(1)}, u32[]{:S(2)}, u32[]{:S(2)}) %collective-permute-start.36) | collective-permute-done | bytes 368672 | tf_op jit(solution)/shard_map/ppermute | solution.py:1063
  247.9 1.3 add_convert_fusion.9
  249.2 1.6 collective-permute-start.35
  253.0 6.0 %collective-permute-done.35 = bf16[192,768]{1,0:T(8,128)(2,1)S(1)} collective-permute-done((bf16[192,768]{1,0:T(8,128)(2,1)S(1)}, bf16[192,768]{1,0:T(8,128)(2,1)S(1)}, u32[]{:S(2)}, u32[]{:S(2)}) %collective-permute-start.35) | collective-permute-done | bytes 294944 | tf_op jit(solution)/shard_map/ppermute | solution.py:1063
  259.1 3.7 %collective-permute-done.38 = bf16[192,512]{1,0:T(8,128)(2,1)S(1)} collective-permute-done((bf16[192,512]{1,0:T(8,128)(2,1)S(1)}, bf16[192,512]{1,0:T(8,128)(2,1)S(1)}, u32[]{:S(2)}, u32[]{:S(2)}) %collective-permute-start.38) | collective-permute-done | bytes 196640 | tf_op jit(solution)/shard_map/ppermute | solution.py:1063
  263.8 6.6 %collective-permute-done.39 = bf16[96,1280]{1,0:T(8,128)(2,1)S(1)} collective-permute-done((bf16[96,1280]{1,0:T(8,128)(2,1)S(1)}, bf16[96,1280]{1,0:T(8,128)(2,1)S(1)}, u32[]{:S(2)}, u32[]{:S(2)}) %collective-permute-start.39) | collective-permute-done | bytes 245792 | tf_op jit(solution)/shard_map/ppermute | solution.py:1063
  271.0 8.1 %collective-permute-done.42 = bf16[48,3840]{1,0:T(8,128)(2,1)S(1)} collective-permute-done((bf16[48,3840]{1,0:T(8,128)(2,1)S(1)}, bf16[48,3840]{1,0:T(8,128)(2,1)S(1)}, u32[]{:S(2)}, u32[]{:S(2)}) %collective-permute-start.42) | collective-permute-done | bytes 368672 | tf_op jit(solution)/shard_map/ppermute | solution.py:1066
  281.4 1.3 add_bitcast_fusion
  282.7 3.1 %collective-permute-done.41 = bf16[48,1280]{1,0:T(8,128)(2,1)S(1)} collective-permute-done((bf16[48,1280]{1,0:T(8,128)(2,1)S(1)}, bf16[48,1280]{1,0:T(8,128)(2,1)S(1)}, u32[]{:S(2)}, u32[]{:S(2)}) %collective-permute-start.41) | collective-permute-done | bytes 122912 | tf_op jit(solution)/shard_map/ppermute | solution.py:1066
  288.7 1.1 reshape.142
  (193 shorter events, 30.0 us)
Async XLA Ops:
  0.7 1.8 copy-start.30
  0.7 6.1 %copy-start.17 = (f32[192,768]{1,0:T(8,128)S(1)}, f32[192,768]{1,0:T(8,128)}, u32[]{:S(2)}) copy-start(f32[192,768]{1,0:T(8,128)} %param.28) | copy-start | bytes 1769476
  0.7 7.7 %copy-start.36 = (s32[1,2]{1,0:T(1,128)S(1)}, s32[1,2]{1,0:T(1,128)}, u32[]{:S(2)}) copy-start(s32[1,2]{1,0:T(1,128)} %param.18) | copy-start | bytes 28
  0.8 9.7 %copy-start.18 = (f32[48,3072]{1,0:T(8,128)S(1)}, f32[48,3072]{1,0:T(8,128)}, u32[]{:S(2)}) copy-start(f32[48,3072]{1,0:T(8,128)} %param.26) | copy-start | bytes 1769476
  2.2 8.3 %copy-start.23 = (f32[48,768]{1,0:T(8,128)S(1)}, f32[48,768]{1,0:T(8,128)}, u32[]{:S(2)}) copy-start(f32[48,768]{1,0:T(8,128)} %param.22) | copy-start | bytes 442372
  2.7 10.1 %collective-permute-start.1 = (bf16[48,1280]{1,0:T(8,128)(2,1)S(1)}, bf16[48,1280]{1,0:T(8,128)(2,1)S(1)}, u32[]{:S(2)}, u32[]{:S(2)}) collective-permute-start(bf16[48,1280]{1,0:T(8,128)(2,1)S(1)} %pad_maximum_fusion.7), channel_id=1, source_target_pairs={{0,8},{1,9},{2,10},{3,11},{4,12},{5,13},{6,14},{7,15},{8,0},{9,1},... | collective-permute-start | bytes 368648 | tf_op jit(solution)/shard_map/ppermute | solution.py:1063
  6.9 36.8 %collective-permute-start.6 = (bf16[192,768]{1,0:T(8,128)(2,1)S(1)}, bf16[192,768]{1,0:T(8,128)(2,1)}, u32[]{:S(2)}, u32[]{:S(2)}) collective-permute-start(bf16[192,768]{1,0:T(8,128)(2,1)S(1)} %convert_element_type.242), channel_id=1, source_target_pairs={{0,2},{1,3},{2,0},{3,1},{4,6},{5,7},{6,4},{7,5},{8,10},{9,11},{10,... | collective-permute-start | bytes 884744 | tf_op jit(solution)/shard_map/ppermute | solution.py:1063
  8.4 3.5 %collective-permute-start = (s32[1,2]{1,0:T(1,128)S(1)}, s32[1,2]{1,0:T(1,128)S(1)}, u32[]{:S(2)}, u32[]{:S(2)}) collective-permute-start(s32[1,2]{1,0:T(1,128)S(1)} %copy-done.36), channel_id=1, source_target_pairs={{0,16},{16,0},{1,17},{17,1},{2,18},{18,2},{3,19},{19,3},{4,20},{20... | collective-permute-start | bytes 32 | tf_op jit(solution)/shard_map/ppermute | solution.py:1066
  10.0 37.1 %collective-permute-start.7 = (bf16[512,768]{1,0:T(8,128)(2,1)}, bf16[512,768]{1,0:T(8,128)(2,1)}, u32[]{:S(2)}, u32[]{:S(2)}) collective-permute-start(bf16[512,768]{1,0:T(8,128)(2,1)} %bitcast.31.rest_0_.rest_4_), channel_id=1, source_target_pairs={{0,16},{16,0},{1,17},{17,1},{2,18},{18,2},{3,19},{19,3},{4,20},{20... | collective-permute-start | bytes 2359304 | tf_op jit(solution)/shard_map/ppermute | solution.py:1066
  10.5 18.2 %copy-start.19 = (bf16[48,1536]{1,0:T(8,128)(2,1)}, bf16[48,1536]{1,0:T(8,128)(2,1)S(1)}, u32[]{:S(2)}) copy-start(bf16[48,1536]{1,0:T(8,128)(2,1)S(1)} %get-tuple-element.89) | copy-start | bytes 442372
  12.8 11.9 %collective-permute-start.3 = (bf16[96,1280]{1,0:T(8,128)(2,1)S(1)}, bf16[96,1280]{1,0:T(8,128)(2,1)S(1)}, u32[]{:S(2)}, u32[]{:S(2)}) collective-permute-start(bf16[96,1280]{1,0:T(8,128)(2,1)S(1)} %pad_maximum_fusion.3), channel_id=1, source_target_pairs={{0,4},{1,5},{2,6},{3,7},{4,0},{5,1},{6,2},{7,3},{8,12},{9,13},{10,... | collective-permute-start | bytes 737288 | tf_op jit(solution)/shard_map/ppermute | solution.py:1063
  13.7 10.1 %collective-permute-start.2 = (bf16[48,2304]{1,0:T(8,128)(2,1)S(1)}, bf16[48,2304]{1,0:T(8,128)(2,1)S(1)}, u32[]{:S(2)}, u32[]{:S(2)}) collective-permute-start(bf16[48,2304]{1,0:T(8,128)(2,1)S(1)} %pad_maximum_fusion.5), channel_id=1, source_target_pairs={{0,8},{1,9},{2,10},{3,11},{4,12},{5,13},{6,14},{7,15},{8,0},{9,1},... | collective-permute-start | bytes 663560 | tf_op jit(solution)/shard_map/ppermute | solution.py:1063
  24.8 22.2 %copy-start.1 = (bf16[192,1280]{1,0:T(8,128)(2,1)}, bf16[192,1280]{1,0:T(8,128)(2,1)S(1)}, u32[]{:S(2)}) copy-start(bf16[192,1280]{1,0:T(8,128)(2,1)S(1)} %pad_maximum_fusion.1.rest_3_.rest_7_.rest_1_.rest_0_) | copy-start | bytes 1474564
  24.8 16.2 %collective-permute-start.4 = (bf16[96,2304]{1,0:T(8,128)(2,1)S(1)}, bf16[96,2304]{1,0:T(8,128)(2,1)S(1)}, u32[]{:S(2)}, u32[]{:S(2)}) collective-permute-start(bf16[96,2304]{1,0:T(8,128)(2,1)S(1)} %constant_dynamic-update-slice_fusion), channel_id=1, source_target_pairs={{0,4},{1,5},{2,6},{3,7},{4,0},{5,1},{6,2},{7,3},{8,12},{9,13},{10,... | collective-permute-start | bytes 1327112 | tf_op jit(solution)/shard_map/ppermute | solution.py:1063
  28.8 12.3 %collective-permute-start.5 = (bf16[48,1536]{1,0:T(8,128)(2,1)S(1)}, bf16[48,1536]{1,0:T(8,128)(2,1)S(1)}, u32[]{:S(2)}, u32[]{:S(2)}) collective-permute-start(bf16[48,1536]{1,0:T(8,128)(2,1)S(1)} %get-tuple-element.89), channel_id=1, source_target_pairs={{0,8},{1,9},{2,10},{3,11},{4,12},{5,13},{6,14},{7,15},{8,0},{9,1},... | collective-permute-start | bytes 442376 | tf_op jit(solution)/shard_map/ppermute | solution.py:1063
  31.0 11.8 %copy-start.20 = (bf16[48,1536]{1,0:T(8,128)(2,1)S(1)}, bf16[48,1536]{1,0:T(8,128)(2,1)}, u32[]{:S(2)}) copy-start(bf16[48,1536]{1,0:T(8,128)(2,1)} %copy-done.19) | copy-start | bytes 442372
  31.0 11.7 %collective-permute-start.8 = (bf16[192,1280]{1,0:T(8,128)(2,1)S(1)}, bf16[192,1280]{1,0:T(8,128)(2,1)S(1)}, u32[]{:S(2)}, u32[]{:S(2)}) collective-permute-start(bf16[192,1280]{1,0:T(8,128)(2,1)S(1)} %pad_maximum_fusion.1.rest_3_.rest_7_.rest_1_.rest_0_), channel_id=1, source_target_pairs={{0,2},{1,3},{2,0},{3,1},{4,6},{5,7},{6,4},{7,5},{8,10},{9,11},{10,... | collective-permute-start | bytes 1474568 | tf_op jit(solution)/shard_map/ppermute | solution.py:1063
  41.0 9.8 %collective-permute-start.9 = (bf16[192,1280]{1,0:T(8,128)(2,1)S(1)}, bf16[192,1280]{1,0:T(8,128)(2,1)S(1)}, u32[]{:S(2)}, u32[]{:S(2)}) collective-permute-start(bf16[192,1280]{1,0:T(8,128)(2,1)S(1)} %pad_maximum_fusion.1.rest_3_.rest_7_.rest_1_.rest_0_), channel_id=1, source_target_pairs={{0,1},{1,0},{2,3},{3,2},{4,5},{5,4},{6,7},{7,6},{8,9},{9,8},{10,11... | collective-permute-start | bytes 1474568 | tf_op jit(solution)/shard_map/ppermute | solution.py:1063
  41.0 32.6 %copy-start = (bf16[192,2304]{1,0:T(8,128)(2,1)}, bf16[192,2304]{1,0:T(8,128)(2,1)S(1)}, u32[]{:S(2)}) copy-start(bf16[192,2304]{1,0:T(8,128)(2,1)S(1)} %constant_dynamic-update-slice_fusion.2.rest_0_.rest_11_.rest_8_.rest_16_) | copy-start | bytes 2654212
  41.1 32.7 %collective-permute-start.12 = (bf16[192,2304]{1,0:T(8,128)(2,1)S(1)}, bf16[192,2304]{1,0:T(8,128)(2,1)S(1)}, u32[]{:S(2)}, u32[]{:S(2)}) collective-permute-start(bf16[192,2304]{1,0:T(8,128)(2,1)S(1)} %constant_dynamic-update-slice_fusion.2.rest_0_.rest_11_.rest_8_.rest_16_), channel_id=1, source_target_pairs={{0,2},{1,3},{2,0},{3,1},{4,6},{5,7},{6,4},{7,5},{8,10},{9,11},{10,... | collective-permute-start | bytes 2654216 | tf_op jit(solution)/shard_map/ppermute | solution.py:1063
  42.8 8.0 %copy-start.4 = (bf16[192,1280]{1,0:T(8,128)(2,1)}, bf16[192,1280]{1,0:T(8,128)(2,1)S(1)}, u32[]{:S(2)}) copy-start(bf16[192,1280]{1,0:T(8,128)(2,1)S(1)} %collective-permute-done.8.rest_4_.rest_8_.rest_2_.rest_1_) | copy-start | bytes 1474564
  42.8 8.0 %collective-permute-start.10 = (bf16[192,1280]{1,0:T(8,128)(2,1)S(1)}, bf16[192,1280]{1,0:T(8,128)(2,1)S(1)}, u32[]{:S(2)}, u32[]{:S(2)}) collective-permute-start(bf16[192,1280]{1,0:T(8,128)(2,1)S(1)} %collective-permute-done.8.rest_4_.rest_8_.rest_2_.rest_1_), channel_id=1, source_target_pairs={{0,1},{1,0},{2,3},{3,2},{4,5},{5,4},{6,7},{7,6},{8,9},{9,8},{10,11... | collective-permute-start | bytes 1474568 | tf_op jit(solution)/shard_map/ppermute | solution.py:1063
  43.6 21.8 %collective-permute-start.11 = (bf16[96,1536]{1,0:T(8,128)(2,1)}, bf16[96,1536]{1,0:T(8,128)(2,1)}, u32[]{:S(2)}, u32[]{:S(2)}) collective-permute-start(bf16[96,1536]{1,0:T(8,128)(2,1)} %pad_maximum_fusion.2), channel_id=1, source_target_pairs={{0,4},{1,5},{2,6},{3,7},{4,0},{5,1},{6,2},{7,3},{8,12},{9,13},{10,... | collective-permute-start | bytes 884744 | tf_op jit(solution)/shard_map/ppermute | solution.py:1063
  47.0 29.3 %collective-permute-start.17 = (bf16[384,768]{1,0:T(8,128)(2,1)}, bf16[384,768]{1,0:T(8,128)(2,1)}, u32[]{:S(2)}, u32[]{:S(2)}) collective-permute-start(bf16[384,768]{1,0:T(8,128)(2,1)} %pad_maximum_fusion), channel_id=1, source_target_pairs={{0,8},{1,9},{2,10},{3,11},{4,12},{5,13},{6,14},{7,15},{8,0},{9,1},... | collective-permute-start | bytes 1769480 | tf_op jit(solution)/shard_map/ppermute | solution.py:1063
  63.8 9.9 %collective-permute-start.13 = (bf16[512,256]{1,0:T(8,128)(2,1)}, bf16[512,256]{1,0:T(8,128)(2,1)S(1)}, u32[]{:S(2)}, u32[]{:S(2)}) collective-permute-start(bf16[512,256]{1,0:T(8,128)(2,1)} %get-tuple-element.94), channel_id=1, source_target_pairs={{0,16},{16,0},{1,17},{17,1},{2,18},{18,2},{3,19},{19,3},{4,20},{20... | collective-permute-start | bytes 786440 | tf_op jit(solution)/shard_map/ppermute | solution.py:1066
  73.6 5.8 %copy-start.33 = (bf16[512,128]{1,0:T(8,128)(2,1)S(1)}, bf16[512,128]{1,0:T(8,128)(2,1)}, u32[]{:S(2)}) copy-start(bf16[512,128]{1,0:T(8,128)(2,1)} %get-tuple-element.98) | copy-start | bytes 393220
  73.6 11.0 %collective-permute-start.15 = (bf16[192,2304]{1,0:T(8,128)(2,1)S(1)}, bf16[192,2304]{1,0:T(8,128)(2,1)S(1)}, u32[]{:S(2)}, u32[]{:S(2)}) collective-permute-start(bf16[192,2304]{1,0:T(8,128)(2,1)S(1)} %constant_dynamic-update-slice_fusion.2.rest_0_.rest_11_.rest_8_.rest_16_), channel_id=1, source_target_pairs={{0,1},{1,0},{2,3},{3,2},{4,5},{5,4},{6,7},{7,6},{8,9},{9,8},{10,11... | collective-permute-start | bytes 2654216 | tf_op jit(solution)/shard_map/ppermute | solution.py:1063
  73.7 10.9 %copy-start.15 = (bf16[512,256]{1,0:T(8,128)(2,1)}, bf16[512,256]{1,0:T(8,128)(2,1)S(1)}, u32[]{:S(2)}) copy-start(bf16[512,256]{1,0:T(8,128)(2,1)S(1)} %collective-permute-done.13.rest_8_.rest_2_) | copy-start | bytes 786436
  73.8 10.9 %copy-start.2 = (bf16[192,2304]{1,0:T(8,128)(2,1)}, bf16[192,2304]{1,0:T(8,128)(2,1)S(1)}, u32[]{:S(2)}) copy-start(bf16[192,2304]{1,0:T(8,128)(2,1)S(1)} %collective-permute-done.12.rest_1_.rest_12_.rest_9_.rest_17_) | copy-start | bytes 2654212
  73.8 10.8 %collective-permute-start.16 = (bf16[192,2304]{1,0:T(8,128)(2,1)S(1)}, bf16[192,2304]{1,0:T(8,128)(2,1)}, u32[]{:S(2)}, u32[]{:S(2)}) collective-permute-start(bf16[192,2304]{1,0:T(8,128)(2,1)S(1)} %collective-permute-done.12.rest_1_.rest_12_.rest_9_.rest_17_), channel_id=1, source_target_pairs={{0,1},{1,0},{2,3},{3,2},{4,5},{5,4},{6,7},{7,6},{8,9},{9,8},{10,11... | collective-permute-start | bytes 2654216 | tf_op jit(solution)/shard_map/ppermute | solution.py:1063
  76.3 20.1 %collective-permute-start.14 = (bf16[192,1536]{1,0:T(8,128)(2,1)}, bf16[192,1536]{1,0:T(8,128)(2,1)}, u32[]{:S(2)}, u32[]{:S(2)}) collective-permute-start(bf16[192,1536]{1,0:T(8,128)(2,1)} %constant_dynamic-update-slice_fusion.4.rest_0_.rest_12_), channel_id=1, source_target_pairs={{0,2},{1,3},{2,0},{3,1},{4,6},{5,7},{6,4},{7,5},{8,10},{9,11},{10,... | collective-permute-start | bytes 1769480 | tf_op jit(solution)/shard_map/ppermute | solution.py:1063
  78.8 29.8 %collective-permute-start.21 = (bf16[768,768]{1,0:T(8,128)(2,1)}, bf16[768,768]{1,0:T(8,128)(2,1)}, u32[]{:S(2)}, u32[]{:S(2)}) collective-permute-start(bf16[768,768]{1,0:T(8,128)(2,1)} %constant_dynamic-update-slice_fusion.6.rest_0_.rest_4_), channel_id=1, source_target_pairs={{0,4},{1,5},{2,6},{3,7},{4,0},{5,1},{6,2},{7,3},{8,12},{9,13},{10,... | collective-permute-start | bytes 3538952 | tf_op jit(solution)/shard_map/ppermute | solution.py:1063
  79.4 5.2 %collective-permute-start.18 = (bf16[512,128]{1,0:T(8,128)(2,1)S(1)}, bf16[512,128]{1,0:T(8,128)(2,1)S(1)}, u32[]{:S(2)}, u32[]{:S(2)}) collective-permute-start(bf16[512,128]{1,0:T(8,128)(2,1)S(1)} %copy-done.33), channel_id=1, source_target_pairs={{0,16},{16,0},{1,17},{17,1},{2,18},{18,2},{3,19},{19,3},{4,20},{20... | collective-permute-start | bytes 393224 | tf_op jit(solution)/shard_map/ppermute | solution.py:1066
  96.5 2.3 collective-permute-start.19
  96.6 3.0 %collective-permute-start.20 = (bf16[192,1536]{1,0:T(8,128)(2,1)}, bf16[192,1536]{1,0:T(8,128)(2,1)S(1)}, u32[]{:S(2)}, u32[]{:S(2)}) collective-permute-start(bf16[192,1536]{1,0:T(8,128)(2,1)} %collective-permute-done.14.rest_1_.rest_13_), channel_id=1, source_target_pairs={{0,1},{1,0},{2,3},{3,2},{4,5},{5,4},{6,7},{7,6},{8,9},{9,8},{10,11... | collective-permute-start | bytes 1769480 | tf_op jit(solution)/shard_map/ppermute | solution.py:1063
  108.6 3.1 %collective-permute-start.22 = (bf16[768,768]{1,0:T(8,128)(2,1)}, bf16[768,768]{1,0:T(8,128)(2,1)S(1)}, u32[]{:S(2)}, u32[]{:S(2)}) collective-permute-start(bf16[768,768]{1,0:T(8,128)(2,1)} %constant_dynamic-update-slice_fusion.6.rest_0_.rest_4_), channel_id=1, source_target_pairs={{0,1},{1,0},{2,3},{3,2},{4,5},{5,4},{6,7},{7,6},{8,9},{9,8},{10,11... | collective-permute-start | bytes 3538952 | tf_op jit(solution)/shard_map/ppermute | solution.py:1063
  108.8 4.6 %collective-permute-start.23 = (bf16[768,768]{1,0:T(8,128)(2,1)}, bf16[768,768]{1,0:T(8,128)(2,1)S(1)}, u32[]{:S(2)}, u32[]{:S(2)}) collective-permute-start(bf16[768,768]{1,0:T(8,128)(2,1)} %collective-permute-done.21.rest_1_.rest_5_), channel_id=1, source_target_pairs={{0,1},{1,0},{2,3},{3,2},{4,5},{5,4},{6,7},{7,6},{8,9},{9,8},{10,11... | collective-permute-start | bytes 3538952 | tf_op jit(solution)/shard_map/ppermute | solution.py:1063
  132.0 4.8 %collective-permute-start.24 = (bf16[1536,768]{1,0:T(8,128)(2,1)}, bf16[1536,768]{1,0:T(8,128)(2,1)S(1)}, u32[]{:S(2)}, u32[]{:S(2)}) collective-permute-start(bf16[1536,768]{1,0:T(8,128)(2,1)} %get-tuple-element.120), channel_id=1, source_target_pairs={{0,1},{1,0},{2,3},{3,2},{4,5},{5,4},{6,7},{7,6},{8,9},{9,8},{10,11... | collective-permute-start | bytes 7077896 | tf_op jit(solution)/shard_map/ppermute | solution.py:1063
  139.0 28.1 %collective-permute-start.25 = (bf16[768,768]{1,0:T(8,128)(2,1)S(1)}, bf16[768,768]{1,0:T(8,128)(2,1)S(1)}, u32[]{:S(2)}, u32[]{:S(2)}) collective-permute-start(bf16[768,768]{1,0:T(8,128)(2,1)S(1)} %get-tuple-element.253), channel_id=1, source_target_pairs={{0,4},{1,5},{2,6},{3,7},{4,0},{5,1},{6,2},{7,3},{8,12},{9,13},{10,... | collective-permute-start | bytes 3538952 | tf_op jit(solution)/shard_map/ppermute | solution.py:1063
  167.1 5.6 %collective-permute-start.26 = (bf16[384,3840]{1,0:T(8,128)(2,1)}, bf16[384,3840]{1,0:T(8,128)(2,1)S(1)}, u32[]{:S(2)}, u32[]{:S(2)}) collective-permute-start(bf16[384,3840]{1,0:T(8,128)(2,1)} %get-tuple-element.129), channel_id=1, source_target_pairs={{0,1},{1,0},{2,3},{3,2},{4,5},{5,4},{6,7},{7,6},{8,9},{9,8},{10,11... | collective-permute-start | bytes 8847368 | tf_op jit(solution)/shard_map/ppermute | solution.py:1063
  175.3 2.8 copy-start.32
  175.3 3.7 %copy-start.14 = (bf16[768,768]{1,0:T(8,128)(2,1)S(1)}, bf16[768,768]{1,0:T(8,128)(2,1)}, u32[]{:S(2)}) copy-start(bf16[768,768]{1,0:T(8,128)(2,1)} %copy-done.13) | copy-start | bytes 3538948
  176.5 24.6 %collective-permute-start.27 = (bf16[96,3840]{1,0:T(8,128)(2,1)}, bf16[96,3840]{1,0:T(8,128)(2,1)}, u32[]{:S(2)}, u32[]{:S(2)}) collective-permute-start(bf16[96,3840]{1,0:T(8,128)(2,1)} %get-tuple-element.257), channel_id=1, source_target_pairs={{0,2},{1,3},{2,0},{3,1},{4,6},{5,7},{6,4},{7,5},{8,10},{9,11},{10,... | collective-permute-start | bytes 2211848 | tf_op jit(solution)/shard_map/ppermute | solution.py:1063
  178.1 10.9 %collective-permute-start.28 = (bf16[512,384]{1,0:T(8,128)(2,1)S(1)}, bf16[512,384]{1,0:T(8,128)(2,1)S(1)}, u32[]{:S(2)}, u32[]{:S(2)}) collective-permute-start(bf16[512,384]{1,0:T(8,128)(2,1)S(1)} %copy-done.32), channel_id=1, source_target_pairs={{0,16},{16,0},{1,17},{17,1},{2,18},{18,2},{3,19},{19,3},{4,20},{20... | collective-permute-start | bytes 1179656 | tf_op jit(solution)/shard_map/ppermute | solution.py:1066
  180.1 28.8 %collective-permute-start.29 = (bf16[384,768]{1,0:T(8,128)(2,1)}, bf16[384,768]{1,0:T(8,128)(2,1)}, u32[]{:S(2)}, u32[]{:S(2)}) collective-permute-start(bf16[384,768]{1,0:T(8,128)(2,1)} %get-tuple-element.255), channel_id=1, source_target_pairs={{0,8},{1,9},{2,10},{3,11},{4,12},{5,13},{6,14},{7,15},{8,0},{9,1},... | collective-permute-start | bytes 1769480 | tf_op jit(solution)/shard_map/ppermute | solution.py:1063
  182.6 44.3 %collective-permute-start.30 = (bf16[96,3840]{1,0:T(8,128)(2,1)}, bf16[96,3840]{1,0:T(8,128)(2,1)}, u32[]{:S(2)}, u32[]{:S(2)}) collective-permute-start(bf16[96,3840]{1,0:T(8,128)(2,1)} %get-tuple-element.256), channel_id=1, source_target_pairs={{0,2},{1,3},{2,0},{3,1},{4,6},{5,7},{6,4},{7,5},{8,10},{9,11},{10,... | collective-permute-start | bytes 2211848 | tf_op jit(solution)/shard_map/ppermute | solution.py:1063
  203.3 23.6 %collective-permute-start.31 = (bf16[96,3840]{1,0:T(8,128)(2,1)}, bf16[96,3840]{1,0:T(8,128)(2,1)S(1)}, u32[]{:S(2)}, u32[]{:S(2)}) collective-permute-start(bf16[96,3840]{1,0:T(8,128)(2,1)} %add_convert_fusion.4), channel_id=1, source_target_pairs={{0,4},{1,5},{2,6},{3,7},{4,0},{5,1},{6,2},{7,3},{8,12},{9,13},{10,... | collective-permute-start | bytes 2211848 | tf_op jit(solution)/shard_map/ppermute | solution.py:1063
  210.8 17.7 %collective-permute-start.32 = (bf16[192,768]{1,0:T(8,128)(2,1)}, bf16[192,768]{1,0:T(8,128)(2,1)}, u32[]{:S(2)}, u32[]{:S(2)}) collective-permute-start(bf16[192,768]{1,0:T(8,128)(2,1)} %get-tuple-element.261), channel_id=1, source_target_pairs={{0,2},{1,3},{2,0},{3,1},{4,6},{5,7},{6,4},{7,5},{8,10},{9,11},{10,... | collective-permute-start | bytes 884744 | tf_op jit(solution)/shard_map/ppermute | solution.py:1063
  226.9 14.6 %collective-permute-start.34 = (bf16[384,768]{1,0:T(8,128)(2,1)}, bf16[384,768]{1,0:T(8,128)(2,1)}, u32[]{:S(2)}, u32[]{:S(2)}) collective-permute-start(bf16[384,768]{1,0:T(8,128)(2,1)} %get-tuple-element.141), channel_id=1, source_target_pairs={{0,1},{1,0},{2,3},{3,2},{4,5},{5,4},{6,7},{7,6},{8,9},{9,8},{10,11... | collective-permute-start | bytes 1769480 | tf_op jit(solution)/shard_map/ppermute | solution.py:1063
  228.3 2.9 copy-start.24
  228.4 19.4 %collective-permute-start.36 = (bf16[48,3840]{1,0:T(8,128)(2,1)S(1)}, bf16[48,3840]{1,0:T(8,128)(2,1)S(1)}, u32[]{:S(2)}, u32[]{:S(2)}) collective-permute-start(bf16[48,3840]{1,0:T(8,128)(2,1)S(1)} %slice.340), channel_id=1, source_target_pairs={{0,8},{1,9},{2,10},{3,11},{4,12},{5,13},{6,14},{7,15},{8,0},{9,1},... | collective-permute-start | bytes 1105928 | tf_op jit(solution)/shard_map/ppermute | solution.py:1063
  229.5 21.2 %collective-permute-start.43 = (bf16[192,768]{1,0:T(8,128)(2,1)S(1)}, bf16[192,768]{1,0:T(8,128)(2,1)S(1)}, u32[]{:S(2)}, u32[]{:S(2)}) collective-permute-start(bf16[192,768]{1,0:T(8,128)(2,1)S(1)} %add_convert_fusion.10), channel_id=1, source_target_pairs={{0,16},{16,0},{1,17},{17,1},{2,18},{18,2},{3,19},{19,3},{4,20},{20... | collective-permute-start | bytes 884744 | tf_op jit(solution)/shard_map/ppermute | solution.py:1066
  232.7 15.2 %copy-start.16 = (bf16[384,768]{1,0:T(8,128)(2,1)S(1)}, bf16[384,768]{1,0:T(8,128)(2,1)}, u32[]{:S(2)}) copy-start(bf16[384,768]{1,0:T(8,128)(2,1)} %get-tuple-element.154) | copy-start | bytes 1769476
  247.8 4.3 %collective-permute-start.37 = (bf16[384,512]{1,0:T(8,128)(2,1)}, bf16[384,512]{1,0:T(8,128)(2,1)S(1)}, u32[]{:S(2)}, u32[]{:S(2)}) collective-permute-start(bf16[384,512]{1,0:T(8,128)(2,1)} %get-tuple-element.159), channel_id=1, source_target_pairs={{0,1},{1,0},{2,3},{3,2},{4,5},{5,4},{6,7},{7,6},{8,9},{9,8},{10,11... | collective-permute-start | bytes 1179656 | tf_op jit(solution)/shard_map/ppermute | solution.py:1063
  247.9 3.7 %copy-start.31 = (bf16[512,768]{1,0:T(8,128)(2,1)S(1)}, bf16[512,768]{1,0:T(8,128)(2,1)}, u32[]{:S(2)}) copy-start(bf16[512,768]{1,0:T(8,128)(2,1)} %get-tuple-element.153) | copy-start | bytes 2359300
  247.9 4.3 %copy-start.22 = (bf16[384,512]{1,0:T(8,128)(2,1)S(1)}, bf16[384,512]{1,0:T(8,128)(2,1)}, u32[]{:S(2)}) copy-start(bf16[384,512]{1,0:T(8,128)(2,1)} %get-tuple-element.155) | copy-start | bytes 1179652
  249.2 9.9 %collective-permute-start.35 = (bf16[192,768]{1,0:T(8,128)(2,1)S(1)}, bf16[192,768]{1,0:T(8,128)(2,1)S(1)}, u32[]{:S(2)}, u32[]{:S(2)}) collective-permute-start(bf16[192,768]{1,0:T(8,128)(2,1)S(1)} %get-tuple-element.259), channel_id=1, source_target_pairs={{0,2},{1,3},{2,0},{3,1},{4,6},{5,7},{6,4},{7,5},{8,10},{9,11},{10,... | collective-permute-start | bytes 884744 | tf_op jit(solution)/shard_map/ppermute | solution.py:1063
  251.6 29.7 %collective-permute-start.33 = (bf16[512,768]{1,0:T(8,128)(2,1)S(1)}, bf16[512,768]{1,0:T(8,128)(2,1)S(1)}, u32[]{:S(2)}, u32[]{:S(2)}) collective-permute-start(bf16[512,768]{1,0:T(8,128)(2,1)S(1)} %copy-done.31), channel_id=1, source_target_pairs={{0,16},{16,0},{1,17},{17,1},{2,18},{18,2},{3,19},{19,3},{4,20},{20... | collective-permute-start | bytes 2359304 | tf_op jit(solution)/shard_map/ppermute | solution.py:1066
  252.2 10.6 %collective-permute-start.38 = (bf16[192,512]{1,0:T(8,128)(2,1)S(1)}, bf16[192,512]{1,0:T(8,128)(2,1)S(1)}, u32[]{:S(2)}, u32[]{:S(2)}) collective-permute-start(bf16[192,512]{1,0:T(8,128)(2,1)S(1)} %get-tuple-element.263), channel_id=1, source_target_pairs={{0,2},{1,3},{2,0},{3,1},{4,6},{5,7},{6,4},{7,5},{8,10},{9,11},{10,... | collective-permute-start | bytes 589832 | tf_op jit(solution)/shard_map/ppermute | solution.py:1063
  262.9 7.6 %collective-permute-start.39 = (bf16[96,1280]{1,0:T(8,128)(2,1)S(1)}, bf16[96,1280]{1,0:T(8,128)(2,1)S(1)}, u32[]{:S(2)}, u32[]{:S(2)}) collective-permute-start(bf16[96,1280]{1,0:T(8,128)(2,1)S(1)} %pad_maximum_fusion.4), channel_id=1, source_target_pairs={{0,4},{1,5},{2,6},{3,7},{4,0},{5,1},{6,2},{7,3},{8,12},{9,13},{10,... | collective-permute-start | bytes 737288 | tf_op jit(solution)/shard_map/ppermute | solution.py:1063
  263.0 16.1 %collective-permute-start.42 = (bf16[48,3840]{1,0:T(8,128)(2,1)S(1)}, bf16[48,3840]{1,0:T(8,128)(2,1)S(1)}, u32[]{:S(2)}, u32[]{:S(2)}) collective-permute-start(bf16[48,3840]{1,0:T(8,128)(2,1)S(1)} %add_convert_fusion.7), channel_id=1, source_target_pairs={{0,16},{16,0},{1,17},{17,1},{2,18},{18,2},{3,19},{19,3},{4,20},{20... | collective-permute-start | bytes 1105928 | tf_op jit(solution)/shard_map/ppermute | solution.py:1066
  270.5 10.9 %copy-start.11 = (f32[512,768]{1,0:T(8,128)S(1)}, f32[512,768]{1,0:T(8,128)}, u32[]{:S(2)}) copy-start(f32[512,768]{1,0:T(8,128)} %get-tuple-element.152) | copy-start | bytes 4718596
  270.5 10.2 %collective-permute-start.40 = (bf16[48,1280]{1,0:T(8,128)(2,1)S(1)}, bf16[48,1280]{1,0:T(8,128)(2,1)S(1)}, u32[]{:S(2)}, u32[]{:S(2)}) collective-permute-start(bf16[48,1280]{1,0:T(8,128)(2,1)S(1)} %add_convert_fusion.18), channel_id=1, source_target_pairs={{0,8},{1,9},{2,10},{3,11},{4,12},{5,13},{6,14},{7,15},{8,0},{9,1},... | collective-permute-start | bytes 368648 | tf_op jit(solution)/shard_map/ppermute | solution.py:1063
  280.8 4.9 %collective-permute-start.41 = (bf16[48,1280]{1,0:T(8,128)(2,1)S(1)}, bf16[48,1280]{1,0:T(8,128)(2,1)S(1)}, u32[]{:S(2)}, u32[]{:S(2)}) collective-permute-start(bf16[48,1280]{1,0:T(8,128)(2,1)S(1)} %add_convert_fusion.17), channel_id=1, source_target_pairs={{0,16},{16,0},{1,17},{17,1},{2,18},{18,2},{3,19},{19,3},{4,20},{20... | collective-permute-start | bytes 368648 | tf_op jit(solution)/shard_map/ppermute | solution.py:1066
  (17 other events, 22.0 us)
